TPU v7x, 32 devices: a whole 2x2x4 slice. The times are simulated.
32 devices in a mesh: dom: 8 (over z, y), batch: 4 (over x, core).
Axes of the slice: x: 2, y: 2, z: 4, core: 2. Of those that a mesh axis runs over, the one named last changes fastest.
Arguments:
- signal: bfloat16 [4096, 4, 4, 256], P('dom', 'batch'), may hold values from -6 to 6
- cotangent: bfloat16 [4096, 4, 3, 256], P('dom', 'batch'), may hold values from -6 to 6
- conv_weight: bfloat16 [2, 2, 256, 256], replicated, may hold values from -0.25 to 0.25
- mix_weight: bfloat16 [3, 256, 256], replicated, may hold values from -0.21875 to 0.21875
- send_rows: int32 [64, 16], P('dom'), may hold values from 0 to 511
- send_mask: int32 [64, 16], P('dom'), may hold values 0 or 1
- tile_vals: bfloat16 [128, 128, 128], P('dom'), may hold values from -0.26953125 to 0.26953125
- tile_row: int32 [128], P('dom'), may hold values from 0 to 3
- tile_col: int32 [128], P('dom'), may hold values from 0 to 5
- tile_mask: int32 [128], P('dom'), may hold values 0 or 1
- hub_owner: int32 [8], replicated, may hold values from 0 to 7, as said below
- hub_rows: int32 [8, 16], replicated, may hold values from 0 to 511
Outputs:
- layer_out: bfloat16 [4096, 4, 3, 256], P('dom', 'batch')
- signal_grad: bfloat16 [4096, 4, 4, 256], P('dom', 'batch')
- conv_grad: float32 [2, 2, 256, 256], replicated
- mix_grad: float32 [3, 256, 256], replicated
Inputs may be any that keep to these rules, and one draw needn't show every extreme that they name: `hub_owner`: each owner slot names a different partition.
All inputs are finite; a program needn't handle non-finite values. No bound on the sum of `send_mask` or of `tile_mask` on one device may be relied on, other than what follows from the above.
Results may differ from a plain program's by a relative error of at most 0.0056.
Values may be sent and summed in bfloat16 or wider, within the bound.
A program may use at most 128 MiB of HBM per device.

v0:
```python
import math

import jax
import jax.numpy as jnp
from jax import lax
from jax.sharding import PartitionSpec as P

highest = lax.Precision.HIGHEST


def tile_apply(ext_rows, tile_block, row_ids, col_ids, tile_keep, row_tiles):
    block_rows = tile_block.shape[1]
    features = ext_rows.shape[1]
    chosen = ext_rows.reshape(-1, block_rows, features)[col_ids]
    product = jnp.einsum("tij,tjf->tif", tile_block, chosen, preferred_element_type=jnp.float32)
    product = product * tile_keep[:, None, None]
    onehot = (row_ids[None, :] == jnp.arange(row_tiles, dtype=jnp.int32)[:, None]).astype(
        jnp.float32
    )
    return jnp.einsum("rt,tif->rif", onehot, product, precision=highest).reshape(
        row_tiles * block_rows, features
    )


def tile_back(own_rows, tile_block, row_ids, col_ids, tile_keep, col_tiles):
    block_rows = tile_block.shape[1]
    features = own_rows.shape[1]
    chosen = own_rows.reshape(-1, block_rows, features)[row_ids]
    product = jnp.einsum("tji,tjf->tif", tile_block, chosen, preferred_element_type=jnp.float32)
    product = product * tile_keep[:, None, None]
    onehot = (col_ids[None, :] == jnp.arange(col_tiles, dtype=jnp.int32)[:, None]).astype(
        jnp.float32
    )
    return jnp.einsum("ct,tif->cif", onehot, product, precision=highest).reshape(
        col_tiles * block_rows, features
    )


def mm(left, right):
    return jnp.dot(left, right, preferred_element_type=jnp.float32)


def inner_sum(left, right):
    return lax.dot_general(
        left, right, (((0,), (0,)), ((), ())), preferred_element_type=jnp.float32
    )


def body(
    signal,
    cotangent,
    conv_weight,
    mix_weight,
    send_rows,
    send_mask,
    tile_vals,
    tile_row,
    tile_col,
    tile_mask,
    hub_owner,
    hub_rows,
):
    node_dev, b_dev, steps, chans = signal.shape
    out_steps = steps - 1
    block_rows = tile_vals.shape[1]
    features = b_dev * out_steps * chans
    halo_count = send_rows.shape[0] * send_rows.shape[1]
    hub_count = hub_rows.shape[0] * hub_rows.shape[1]
    ext_count = node_dev + halo_count + hub_count
    my_index = lax.axis_index("dom")
    flat_send = send_rows.reshape(-1)
    send_flag = send_mask.reshape(-1)
    keep_send = send_flag.astype(jnp.bfloat16)
    flat_hub = hub_rows.reshape(-1)
    mine = jnp.repeat(hub_owner, hub_rows.shape[1]) == my_index
    positions = jnp.arange(node_dev, dtype=jnp.int32)
    return_halo = ((positions[:, None] == flat_send[None, :]) & (send_flag[None, :] == 1)).astype(
        jnp.float32
    )
    return_hub = ((positions[:, None] == flat_hub[None, :]) & mine[None, :]).astype(jnp.float32)
    tile_keep = tile_mask.astype(jnp.float32)

    def spread(field):
        outgoing = field[flat_send] * keep_send[:, None]
        incoming = lax.all_to_all(outgoing, "dom", split_axis=0, concat_axis=0, tiled=True)
        placed = jnp.where(
            mine[:, None], field[flat_hub].astype(jnp.float32), jnp.zeros((), jnp.float32)
        )
        hubs = lax.psum(placed, "dom").astype(jnp.bfloat16)
        ext_rows = jnp.concatenate([field, incoming, hubs], 0)
        return tile_apply(
            ext_rows, tile_vals, tile_row, tile_col, tile_keep, node_dev // block_rows
        )

    def gather_back(field):
        ext_grad = tile_back(
            field, tile_vals, tile_row, tile_col, tile_keep, ext_count // block_rows
        )
        returned = lax.all_to_all(
            ext_grad[node_dev : node_dev + halo_count].astype(jnp.bfloat16),
            "dom",
            split_axis=0,
            concat_axis=0,
            tiled=True,
        ).astype(jnp.float32)
        summed = lax.psum(ext_grad[node_dev + halo_count :], "dom")
        local = ext_grad[:node_dev] + jnp.dot(return_halo, returned, precision=highest)
        return local + jnp.dot(return_hub, summed, precision=highest)

    earlier = signal[:, :, :-1, :].reshape(-1, chans)
    later = signal[:, :, 1:, :].reshape(-1, chans)
    filt = mm(earlier, conv_weight[0, 0]) + mm(later, conv_weight[0, 1])
    gate = mm(earlier, conv_weight[1, 0]) + mm(later, conv_weight[1, 1])
    tanh_filt = jnp.tanh(filt)
    sig_gate = jax.nn.sigmoid(gate)
    hidden = (tanh_filt * sig_gate).astype(jnp.bfloat16)
    hop_one = spread(hidden.reshape(node_dev, features)).astype(jnp.bfloat16)
    hop_two = spread(hop_one).astype(jnp.bfloat16)
    hop_one = hop_one.reshape(-1, chans)
    hop_two = hop_two.reshape(-1, chans)
    mixed = (
        later.astype(jnp.float32)
        + mm(hidden, mix_weight[0])
        + mm(hop_one, mix_weight[1])
        + mm(hop_two, mix_weight[2])
    )
    layer_out = mixed.astype(jnp.bfloat16).reshape(node_dev, b_dev, out_steps, chans)
    grad_out = cotangent.reshape(-1, chans)
    mix_part = jnp.stack(
        [inner_sum(hidden, grad_out), inner_sum(hop_one, grad_out), inner_sum(hop_two, grad_out)]
    )
    back_two = mm(grad_out, mix_weight[2].T).astype(jnp.bfloat16)
    back_one = mm(grad_out, mix_weight[1].T) + gather_back(
        back_two.reshape(node_dev, features)
    ).reshape(-1, chans)
    back_one = back_one.astype(jnp.bfloat16)
    grad_hidden = mm(grad_out, mix_weight[0].T) + gather_back(
        back_one.reshape(node_dev, features)
    ).reshape(-1, chans)
    grad_filt = (grad_hidden * sig_gate * (1.0 - tanh_filt * tanh_filt)).astype(jnp.bfloat16)
    grad_gate = (grad_hidden * tanh_filt * sig_gate * (1.0 - sig_gate)).astype(jnp.bfloat16)
    conv_part = jnp.stack(
        [
            jnp.stack([inner_sum(earlier, grad_filt), inner_sum(later, grad_filt)]),
            jnp.stack([inner_sum(earlier, grad_gate), inner_sum(later, grad_gate)]),
        ]
    )
    shape_four = (node_dev, b_dev, out_steps, chans)
    into_earlier = (
        mm(grad_filt, conv_weight[0, 0].T) + mm(grad_gate, conv_weight[1, 0].T)
    ).reshape(shape_four)
    into_later = (
        mm(grad_filt, conv_weight[0, 1].T)
        + mm(grad_gate, conv_weight[1, 1].T)
        + grad_out.astype(jnp.float32)
    ).reshape(shape_four)
    signal_grad = jnp.pad(into_earlier, ((0, 0), (0, 0), (0, 1), (0, 0))) + jnp.pad(
        into_later, ((0, 0), (0, 0), (1, 0), (0, 0))
    )
    conv_total, mix_total = lax.psum((conv_part, mix_part), ("dom", "batch"))
    factor = 1.0 / math.sqrt(
        node_dev * lax.axis_size("dom") * b_dev * lax.axis_size("batch") * out_steps
    )
    return (layer_out, signal_grad.astype(jnp.bfloat16), conv_total * factor, mix_total * factor)


def solution(mesh):
    placed = (
        P("dom", "batch", None, None),
        P("dom", "batch", None, None),
        P(),
        P(),
        P("dom", None),
        P("dom", None),
        P("dom", None, None),
        P("dom"),
        P("dom"),
        P("dom"),
        P(),
        P(),
    )
    return jax.shard_map(
        body,
        mesh=mesh,
        in_specs=placed,
        out_specs=(P("dom", "batch", None, None), P("dom", "batch", None, None), P(), P()),
        check_vma=False,
    )
```

profile of v0, /device:TPU:0, one launch (start us, length us, event | category | flops | bytes accessed | tf_op | source)
XLA Modules:
  0.0 550.5 jit_solution(4992081128185602620)
XLA Ops:
  7.2 1.9 copy.24
  9.8 1.3 convolution_convert_fusion
  11.5 2.4 gather_fusion.6
  14.0 5.6 %fusion.96 = f32[16,768,128]{2,1,0:T(8,128)} fusion(bf16[16,128,768]{2,1,0:T(8,128)(2,1)} %gather_fusion.6, bf16[16,128,128]{2,1,0:T(8,128)(2,1)S(1)} %copy-done), kind=kOutput, calls=%fused_computation.145 | convolution fusion | flops 402653184 | bytes 9961472 | tf_op jit(solution)/shard_map/tji,tjf->tif/dot_general | solution.py:29
  19.6 6.7 %copy.32 = f32[16,768,128]{1,0,2:T(8,128)} copy(f32[16,768,128]{2,1,0:T(8,128)} %fusion.96) | data formatting | bytes 12582912 | tf_op jit(solution)/shard_map/tji,tjf->tif/dot_general | solution.py:29
  26.3 4.6 fusion.2
  30.9 1.6 copy-done.1
  33.8 2.3 slice.168
  36.8 7.3 %all-to-all-start.2 = ((bf16[8,16,768]{2,1,0:T(8,128)(2,1)}), bf16[8,16,768]{2,1,0:T(8,128)(2,1)}, u32[]{:S(2)}, u32[]{:S(2)}) async-start(bf16[8,16,768]{2,1,0:T(8,128)(2,1)} %bitcast.44), calls=%async_computation.2 | async-start | bytes 393216 | tf_op jit(solution)/shard_map/all_to_all | solution.py:99
  44.7 3.3 slice.103
  48.6 3.0 copy.25
  51.6 2.0 fusion.93
  53.7 2.5 reshape.178
  56.2 2.7 reshape.179
  59.3 1.5 fusion.17
  60.8 49.1 %all-reduce.9.cloned.1.call-done = f32[128,768]{1,0:T(8,128)} async-done(((f32[128,768]{1,0:T(8,128)}), f32[128,768]{1,0:T(8,128)}) %all-reduce.9.cloned.1.call-update) | async-done | bytes 393232 | tf_op jit(solution)/shard_map/psum | solution.py:106
  109.9 3.0 fusion.39
  112.9 3.5 fusion.25
  116.4 2.6 reshape.187
  119.0 2.8 fusion.23
  121.8 1.5 reshape_reshape.7
  123.2 2.4 gather_fusion.7
  125.7 5.6 %fusion.97 = f32[16,768,128]{2,1,0:T(8,128)} fusion(bf16[16,128,768]{2,1,0:T(8,128)(2,1)} %gather_fusion.7, bf16[16,128,128]{2,1,0:T(8,128)(2,1)S(1)} %copy-done), kind=kOutput, calls=%fused_computation.146 | convolution fusion | flops 402653184 | bytes 9961472 | tf_op jit(solution)/shard_map/tji,tjf->tif/dot_general | solution.py:29
  131.3 6.7 %copy.33 = f32[16,768,128]{1,0,2:T(8,128)} copy(f32[16,768,128]{2,1,0:T(8,128)} %fusion.97) | data formatting | bytes 12582912 | tf_op jit(solution)/shard_map/tji,tjf->tif/dot_general | solution.py:29
  138.0 4.6 fusion
  142.6 1.6 copy-done.2
  145.4 1.5 fusion.50
  146.9 2.3 slice.167
  149.9 3.8 all-to-all-start.3
  153.7 1.4 slice-done
  155.1 1.5 copy.26
  156.6 60.9 %all-reduce.11.cloned.1.call-done = f32[128,768]{1,0:T(8,128)} async-done(((f32[128,768]{1,0:T(8,128)}), f32[128,768]{1,0:T(8,128)}) %all-reduce.11.cloned.1.call-update) | async-done | bytes 393232 | tf_op jit(solution)/shard_map/psum | solution.py:106
  217.5 3.0 fusion.37
  220.4 3.4 fusion.24
  223.8 2.6 reshape.188
  226.5 2.0 convolution_add_fusion.3
  229.1 1.9 multiply_convert_fusion
  235.5 1.6 fusion.55
  237.1 1.6 fusion.52
  239.0 1.6 gather_fusion.1
  240.6 1.8 convert_select_fusion.1
  242.4 40.9 %all-reduce.14 = bf16[128,768]{1,0:T(8,128)(2,1)} all-reduce(f32[128,768]{1,0:T(8,128)} %convert_select_fusion.1), channel_id=1, replica_groups=mesh['dom'=8,'batch'=4] {'dom'}, use_global_device_ids=true, to_apply=%region_0.1 | all-reduce | flops 98304 | bytes 589824 | tf_op jit(solution)/shard_map/psum | solution.py:89
  283.3 1.5 gather_fusion
  284.8 1.7 broadcast_multiply_fusion.3
  286.5 4.2 all-to-all-start
  290.8 3.4 convolution_add_fusion.1
  294.2 1.6 fusion.16
  296.9 3.6 reshape.189
  300.5 3.6 reshape.190
  304.1 4.0 fusion.32
  310.3 2.4 gather_fusion.2
  312.8 5.6 %fusion.94 = f32[16,768,128]{2,1,0:T(8,128)} fusion(bf16[16,128,768]{2,1,0:T(8,128)(2,1)} %gather_fusion.2, bf16[16,128,128]{2,1,0:T(8,128)(2,1)S(1)} %copy-done), kind=kOutput, calls=%fused_computation.143 | convolution fusion | flops 402653184 | bytes 9961472 | tf_op jit(solution)/shard_map/tij,tjf->tif/dot_general | solution.py:15
  318.3 6.7 %copy.30 = f32[16,768,128]{1,0,2:T(8,128)} copy(f32[16,768,128]{2,1,0:T(8,128)} %fusion.94) | data formatting | bytes 12582912 | tf_op jit(solution)/shard_map/tij,tjf->tif/dot_general | solution.py:15
  325.0 5.6 %fusion.26 = bf16[4,128,768]{2,0,1:T(4,128)(2,1)S(1)} fusion(f32[16,768,128]{1,0,2:T(8,128)} %copy.30, f32[16]{0:T(128)S(1)} %convert_element_type.95, s32[16]{0:T(128)S(1)} %copy-done.30), kind=kOutput, calls=%fused_computation.50 | convolution fusion | flops 77463616 | bytes 7078016 | tf_op jit(solution)/shard_map/rt,tif->rif/dot_general | solution.py:20
  330.7 1.5 gather_fusion.4
  335.5 6.0 %all-to-all-start.1 = ((bf16[8,16,768]{2,1,0:T(8,128)(2,1)}), bf16[8,16,768]{2,1,0:T(8,128)(2,1)S(1)}, u32[]{:S(2)}, u32[]{:S(2)}) async-start(bf16[8,16,768]{2,1,0:T(8,128)(2,1)} %broadcast_multiply_fusion.2), calls=%async_computation.1 | async-start | bytes 393216 | tf_op jit(solution)/shard_map/all_to_all | solution.py:85
  341.5 42.5 %all-reduce.15 = bf16[128,768]{1,0:T(8,128)(2,1)} all-reduce(f32[128,768]{1,0:T(8,128)S(1)} %convert_select_fusion), channel_id=1, replica_groups=mesh['dom'=8,'batch'=4] {'dom'}, use_global_device_ids=true, to_apply=%region_1.2 | all-reduce | flops 98304 | bytes 589824 | tf_op jit(solution)/shard_map/psum | solution.py:89
  386.2 2.4 gather_fusion.5
  388.6 5.6 %fusion.95 = f32[16,768,128]{2,1,0:T(8,128)} fusion(bf16[16,128,768]{2,1,0:T(8,128)(2,1)} %gather_fusion.5, bf16[16,128,128]{2,1,0:T(8,128)(2,1)S(1)} %copy-done), kind=kOutput, calls=%fused_computation.144 | convolution fusion | flops 402653184 | bytes 9961472 | tf_op jit(solution)/shard_map/tij,tjf->tif/dot_general | solution.py:15
  394.2 6.7 %copy.31 = f32[16,768,128]{1,0,2:T(8,128)} copy(f32[16,768,128]{2,1,0:T(8,128)} %fusion.95) | data formatting | bytes 12582912 | tf_op jit(solution)/shard_map/tij,tjf->tif/dot_general | solution.py:15
  400.9 5.6 %fusion.29 = bf16[4,128,768]{2,0,1:T(4,128)(2,1)S(1)} fusion(f32[16,768,128]{1,0,2:T(8,128)} %copy.31, f32[16]{0:T(128)S(1)} %convert_element_type.95, s32[16]{0:T(128)S(1)} %copy-done.30), kind=kOutput, calls=%fused_computation.51 | convolution fusion | flops 77463616 | bytes 7078016 | tf_op jit(solution)/shard_map/rt,tif->rif/dot_general | solution.py:20
  413.0 127.1 %all-reduce.13.cloned.1.call-done = (f32[2,2,256,256]{2,3,1,0:T(8,128)}, f32[3,256,256]{2,1,0:T(8,128)}) async-done(((f32[2,2,256,256]{2,3,1,0:T(8,128)}, f32[3,256,256]{2,1,0:T(8,128)}), (f32[2,2,256,256]{2,3,1,0:T(8,128)}, f32[3,256,256]{2,1,0:T(8,128)})) %all-reduce.13.cloned.1.call-update) | async-done | bytes 1835024 | tf_op jit(solution)/shard_map/psum | solution.py:160
  540.1 1.3 broadcast_multiply_fusion
  541.4 1.3 copy.29
  (129 shorter events, 28.1 us)
Async XLA Ops:
  7.2 6.8 %copy-start = (bf16[16,128,128]{2,1,0:T(8,128)(2,1)S(1)}, bf16[16,128,128]{2,1,0:T(8,128)(2,1)}, u32[]{:S(2)}) copy-start(bf16[16,128,128]{2,1,0:T(8,128)(2,1)} %param.18) | copy-start | bytes 1572868
  7.2 102.8 %all-reduce.9.cloned.1.call-start = ((), (), s32[]{:S(2)}) async-start(), calls=%async_computation.4 | async-start | bytes 786432 | tf_op jit(solution)/shard_map/psum | solution.py:106
  9.8 1.7 copy-start.30
  19.6 6.7 %copy-start.31 = (s32[16]{0:T(128)S(1)}, s32[16]{0:T(128)}, u32[]{:S(2)}) copy-start(s32[16]{0:T(128)} %param.21) | copy-start | bytes 196
  19.6 6.7 %copy-start.29 = (s32[16]{0:T(128)S(1)}, s32[16]{0:T(128)}, u32[]{:S(2)}) copy-start(s32[16]{0:T(128)} %param.20) | copy-start | bytes 196
  30.9 1.6 copy-start.1
  36.8 76.1 %all-to-all-start.2 = ((bf16[8,16,768]{2,1,0:T(8,128)(2,1)}), bf16[8,16,768]{2,1,0:T(8,128)(2,1)}, u32[]{:S(2)}, u32[]{:S(2)}) async-start(bf16[8,16,768]{2,1,0:T(8,128)(2,1)} %bitcast.44), calls=%async_computation.2 | async-start | bytes 393216 | tf_op jit(solution)/shard_map/all_to_all | solution.py:99
  44.1 173.4 %all-reduce.11.cloned.1.call-start = ((), (), s32[]{:S(2)}) async-start(), calls=%async_computation.5 | async-start | bytes 786432 | tf_op jit(solution)/shard_map/psum | solution.py:106
  44.7 3.4 copy-start.27
  44.7 3.5 copy-start.28
  44.7 3.7 copy-start.26
  44.7 3.7 copy-start.32
  48.6 3.1 copy-start.7
  53.7 5.2 copy-start.14
  56.2 3.1 copy-start.3
  142.6 1.6 copy-start.2
  149.9 70.5 %all-to-all-start.3 = ((bf16[8,16,768]{2,1,0:T(8,128)(2,1)}), bf16[8,16,768]{2,1,0:T(8,128)(2,1)S(1)}, u32[]{:S(2)}, u32[]{:S(2)}) async-start(bf16[8,16,768]{2,1,0:T(8,128)(2,1)} %bitcast.46), calls=%async_computation.3 | async-start | bytes 393216 | tf_op jit(solution)/shard_map/all_to_all | solution.py:99
  153.7 1.4 slice-start
  226.5 2.0 copy-start.4
  226.5 2.2 copy-start.15
  226.5 2.7 copy-start.17
  231.1 2.2 copy-start.10
  237.1 1.6 copy-start.8
  286.5 22.8 %all-to-all-start = ((bf16[8,16,768]{2,1,0:T(8,128)(2,1)}), bf16[8,16,768]{2,1,0:T(8,128)(2,1)}, u32[]{:S(2)}, u32[]{:S(2)}) async-start(bf16[8,16,768]{2,1,0:T(8,128)(2,1)} %broadcast_multiply_fusion.3), calls=%async_computation | async-start | bytes 393216 | tf_op jit(solution)/shard_map/all_to_all | solution.py:85
  290.8 3.4 copy-start.6
  290.8 3.4 copy-start.11
  294.2 1.6 copy-start.22
  294.2 1.6 copy-start.23
  294.2 1.6 copy-start.24
  294.2 1.6 copy-start.25
  308.2 1.1 copy-start.19
  333.5 51.7 %copy-start.12 = (bf16[1536,256]{1,0:T(8,128)(2,1)}, bf16[1536,256]{1,0:T(8,128)(2,1)S(1)}, u32[]{:S(2)}) copy-start(bf16[1536,256]{1,0:T(8,128)(2,1)S(1)} %convert_element_type.97) | copy-start | bytes 2359300
  335.5 49.6 %all-to-all-start.1 = ((bf16[8,16,768]{2,1,0:T(8,128)(2,1)}), bf16[8,16,768]{2,1,0:T(8,128)(2,1)S(1)}, u32[]{:S(2)}, u32[]{:S(2)}) async-start(bf16[8,16,768]{2,1,0:T(8,128)(2,1)} %broadcast_multiply_fusion.2), calls=%async_computation.1 | async-start | bytes 393216 | tf_op jit(solution)/shard_map/all_to_all | solution.py:85
  341.5 198.6 %all-reduce.13.cloned.1.call-start = ((), (), s32[]{:S(2)}) async-start(), calls=%async_computation.6 | async-start | bytes 3670016 | tf_op jit(solution)/shard_map/psum | solution.py:160
  406.6 1.0 copy-start.20
  407.0 1.0 copy-start.21
  408.0 1.4 copy-start.5
  408.0 1.7 copy-start.9
  408.0 1.7 copy-start.16
  409.7 1.1 copy-start.13
  541.4 1.3 copy-start.18
Sparse Core Ops, SparseCore 0:
  33.9 76.0 all-reduce.8
  145.5 71.8 all-reduce.10
  409.0 130.9 all-reduce.12
where the time goes:
time: 557 us; the launch traced here: 550 us
  waiting for transfers between devices  237 us (43%)
  local copies, waits for them, and re-layouts  94.4 us (17%)
  blocking collectives  83.4 us (15%)
  matrix products  83.2 us (15%)
  starting transfers between devices  21.9 us (4%)
  other arithmetic  15.9 us (3%)
  between operations  14.6 us (3%)
    psum x1, waiting for transfers between devices, body(): conv_total, mix_total = lax.psum((conv_part, mix_part), ('dom', 'batch'))  127 us
    psum x2, waiting for transfers between devices, gather_back(): summed = lax.psum(ext_grad[node_dev + halo_count:], 'dom')  110 us
    psum x2, blocking collectives, spread(): hubs = lax.psum(placed, 'dom').astype(jnp.bfloat16)  83.4 us
    dot_general x14, matrix products, mm(): return jnp.dot(left, right, preferred_element_type=jnp.float32)  20.6 us
    dot_general x2, local copies, waits for them, and re-layouts, tile_back(): jnp.einsum('tji,tjf->tif', tile_block, chosen, preferred_element_type=jnp...  13.4 us
    dot_general x2, local copies, waits for them, and re-layouts, tile_apply(): jnp.einsum('tij,tjf->tif', tile_block, chosen, preferred_element_type=jnp...  13.4 us
    unnamed x73, local copies, waits for them, and re-layouts  13.2 us
    dot_general x2, matrix products, tile_apply(): jnp.einsum('rt,tif->rif', onehot, product, precision=highest)  11.2 us
  transfers between devices with their start and end apart: 7, of which 3 were waited for; matrix products, arithmetic and copies ran while one was open for 10% of the time, Pallas kernels for 0%

commit v1 on v0

v1 whole, which is shorter than its diff:
```python
import functools
import math

import jax
import jax.numpy as jnp
from jax import lax
from jax.experimental import pallas as pl
from jax.experimental.pallas import tpu as pltpu
from jax.sharding import PartitionSpec as P

VMEM = pl.BlockSpec(memory_space=pltpu.VMEM)
SMEM = pl.BlockSpec(memory_space=pltpu.SMEM)
F32 = jnp.float32
BF16 = jnp.bfloat16


def nn(left, right):
    return lax.dot_general(left, right, (((1,), (0,)), ((), ())), preferred_element_type=F32)


def nt(left, right):
    return lax.dot_general(left, right, (((1,), (1,)), ((), ())), preferred_element_type=F32)


def tn(left, right):
    return lax.dot_general(left, right, (((0,), (0,)), ((), ())), preferred_element_type=F32)


def fill_taps(conv_ref, taps_ref):
    chans = conv_ref.shape[2]
    for kind in range(2):
        for tap in range(2):
            taps_ref[tap * chans : (tap + 1) * chans, kind * chans : (kind + 1) * chans] = conv_ref[
                kind, tap
            ]


def pre_kernel(
    row_ref,
    col_ref,
    keep_ref,
    sig_ref,
    cot_ref,
    conv_ref,
    mix_ref,
    tile_ref,
    pick_ref,
    place_ref,
    own_ref,
    far_ref,
    send_ref,
    hidden_ref,
    tanh_ref,
    gate_ref,
    back_ref,
    out_ref,
    dense_ref,
    taps_ref,
):
    nodes = own_ref.shape[0]
    tiles, block, _ = tile_ref.shape
    chans = conv_ref.shape[2]
    features = hidden_ref.shape[1]
    own_tiles = nodes // block
    all_tiles = dense_ref.shape[0]

    dense_ref[...] = jnp.zeros_like(dense_ref)
    for t in range(tiles):

        @pl.when(keep_ref[t] == 1)
        def _():
            rows = pl.ds(pl.multiple_of(row_ref[t] * block, block), block)
            dense_ref[col_ref[t], rows, :] += tile_ref[t].astype(F32)

    for c in range(own_tiles):
        own_ref[:, c * block : (c + 1) * block] = dense_ref[c].astype(BF16)
    slots = send_ref.shape[0]
    place = (
        place_ref[...] == lax.broadcasted_iota(jnp.int32, (place_ref.shape[0], slots), 1)
    ).astype(BF16)
    far = nn(dense_ref[own_tiles].astype(BF16), place[:block])
    for c in range(own_tiles + 1, all_tiles):
        at = (c - own_tiles) * block
        far += nn(dense_ref[c].astype(BF16), place[at : at + block])
    far_ref[...] = far.astype(BF16)
    send_ref[...] = (
        pick_ref[...] == lax.broadcasted_iota(jnp.int32, (slots, nodes), 1)
    ).astype(BF16)

    fill_taps(conv_ref, taps_ref)
    for t in range(features // chans):
        at = slice(t * chans, (t + 1) * chans)
        both = nn(sig_ref[:, t * chans : (t + 2) * chans], taps_ref[...])
        tanh_filt = jnp.tanh(both[:, :chans])
        sig_gate = jax.nn.sigmoid(both[:, chans:])
        tanh_ref[:, at] = tanh_filt
        gate_ref[:, at] = sig_gate
        hidden_ref[:, at] = (tanh_filt * sig_gate).astype(BF16)
        back_ref[:, at] = nt(cot_ref[:, at], mix_ref[2]).astype(BF16)
    out_ref[:, :features] = nn(send_ref[...], hidden_ref[...]).astype(BF16)
    out_ref[:, features:] = tn(far_ref[...], back_ref[...]).astype(BF16)


def mid_kernel(
    own_ref,
    far_ref,
    send_ref,
    hidden_ref,
    back_ref,
    cot_ref,
    mix_ref,
    in_ref,
    hop_ref,
    next_ref,
    out_ref,
):
    features = hidden_ref.shape[1]
    chans = mix_ref.shape[1]
    for t in range(features // chans):
        at = slice(t * chans, (t + 1) * chans)
        late = slice(features + t * chans, features + (t + 1) * chans)
        hop_ref[:, at] = (
            nn(own_ref[...], hidden_ref[:, at]) + nn(far_ref[...], in_ref[:, at])
        ).astype(BF16)
        next_ref[:, at] = (
            nt(cot_ref[:, at], mix_ref[1])
            + tn(own_ref[...], back_ref[:, at])
            + tn(send_ref[...], in_ref[:, late])
        ).astype(BF16)
    out_ref[:, :features] = nn(send_ref[...], hop_ref[...]).astype(BF16)
    out_ref[:, features:] = tn(far_ref[...], next_ref[...]).astype(BF16)


def post_kernel(
    own_ref,
    far_ref,
    send_ref,
    hidden_ref,
    hop_ref,
    back_ref,
    in_ref,
    sig_ref,
    cot_ref,
    tanh_ref,
    gate_ref,
    conv_ref,
    mix_ref,
    layer_ref,
    grad_ref,
    weight_ref,
    taps_ref,
    last_ref,
    held_ref,
):
    features = hidden_ref.shape[1]
    chans = mix_ref.shape[1]
    steps = features // chans
    fill_taps(conv_ref, taps_ref)
    for t in range(steps):
        at = slice(t * chans, (t + 1) * chans)
        after = slice((t + 1) * chans, (t + 2) * chans)
        late = slice(features + t * chans, features + (t + 1) * chans)
        cot = cot_ref[:, at]
        last_ref[...] = (
            nn(own_ref[...], hop_ref[:, at]) + nn(far_ref[...], in_ref[:, at])
        ).astype(BF16)
        layer_ref[:, at] = (
            sig_ref[:, after].astype(F32)
            + nn(hidden_ref[:, at], mix_ref[0])
            + nn(hop_ref[:, at], mix_ref[1])
            + nn(last_ref[...], mix_ref[2])
        ).astype(BF16)
        for k, source in enumerate((hidden_ref[:, at], hop_ref[:, at], last_ref[...])):
            part = tn(source, cot)
            place = slice((4 + k) * chans, (5 + k) * chans)
            weight_ref[place, :] = part if t == 0 else weight_ref[place, :] + part
        grad_hidden = (
            nt(cot, mix_ref[0])
            + tn(own_ref[...], back_ref[:, at])
            + tn(send_ref[...], in_ref[:, late])
        )
        tanh_filt = tanh_ref[:, at]
        sig_gate = gate_ref[:, at]
        held_ref[:, :chans] = (
            grad_hidden * sig_gate * (1.0 - tanh_filt * tanh_filt)
        ).astype(BF16)
        held_ref[:, chans:] = (grad_hidden * tanh_filt * sig_gate * (1.0 - sig_gate)).astype(BF16)
        outer = tn(sig_ref[:, t * chans : (t + 2) * chans], held_ref[...])
        for kind in range(2):
            for tap in range(2):
                part = outer[tap * chans : (tap + 1) * chans, kind * chans : (kind + 1) * chans]
                spot = (kind * 2 + tap) * chans
                place = slice(spot, spot + chans)
                weight_ref[place, :] = part if t == 0 else weight_ref[place, :] + part
        into = nt(held_ref[...], taps_ref[...])
        early = into[:, :chans]
        if t > 0:
            early = early + carried
        grad_ref[:, at] = early.astype(BF16)
        carried = into[:, chans:] + cot.astype(F32)
    grad_ref[:, features:] = carried.astype(BF16)


def stages_of(axis_sizes):
    bits = {}
    for axis, size in axis_sizes:
        bit = 1
        while bit < size:
            bits.setdefault(axis, []).append((axis, bit))
            bit *= 2
    return bits


def colours_of(bits, rows, chans):
    dom, batch = bits["dom"], bits["batch"]
    first, far = batch[:1], batch[1:]
    near, high = dom[:1], dom[1:]
    orders = (
        first + far + near + high,
        first + near + high + far,
        first + high + far + near,
    )
    units = rows // chans
    shares = [units - 2 * (units // 3), units // 3, units // 3]
    colours, base = [], 0
    for order, share in zip(orders, shares):
        plan, count = [], share * chans
        for axis, bit in order:
            halve = (count // 2) % 8 == 0
            plan.append((axis, bit, halve, count // 2 if halve else count))
            if halve:
                count //= 2
        colours.append((base, share * chans, plan))
        base += share * chans
    return colours


def partner_of(axis, bit):
    index = lax.axis_index(axis)
    mine = (index // bit) % 2
    return mine, index + bit - 2 * bit * mine


def reduce_kernel(
    colours, factor, grads_ref, out_ref, total, landing, send_sem, recv_sem, back_send, back_recv
):
    barrier = pltpu.get_barrier_semaphore()
    peers = sorted({(axis, bit) for axis, bit, _, _ in colours[0][2]})
    for axis, bit in peers:
        _, other = partner_of(axis, bit)
        pl.semaphore_signal(
            barrier, inc=1, device_id={axis: other}, device_id_type=pl.DeviceIdType.MESH
        )
    pl.semaphore_wait(barrier, len(peers))

    starts = [base for base, _, _ in colours]
    trail = [[] for _ in colours]
    landed = 0
    for s in range(len(colours[0][2])):
        moves = []
        for c, (_, _, plan) in enumerate(colours):
            axis, bit, halve, count = plan[s]
            mine, other = partner_of(axis, bit)
            source = grads_ref if s == 0 else total
            keep = starts[c] + mine * count if halve else starts[c]
            give = starts[c] + (1 - mine) * count if halve else starts[c]
            give_rows = pl.ds(pl.multiple_of(give, 8), count)
            keep_rows = pl.ds(pl.multiple_of(keep, 8), count)
            copy = pltpu.make_async_remote_copy(
                src_ref=source.at[give_rows],
                dst_ref=landing.at[pl.ds(landed, count)],
                send_sem=send_sem.at[c, s],
                recv_sem=recv_sem.at[c, s],
                device_id={axis: other},
                device_id_type=pl.DeviceIdType.MESH,
            )
            copy.start()
            moves.append((copy, source, keep_rows, landed, count))
            landed += count
            trail[c].append(keep)
            starts[c] = keep
        for copy, source, keep_rows, at, count in moves:
            copy.wait()
            total[keep_rows, :] = source[keep_rows, :] + landing[at : at + count, :]

    counts = []
    for c, (_, _, plan) in enumerate(colours):
        count = plan[-1][3]
        rows = pl.ds(pl.multiple_of(starts[c], 8), count)
        out_ref[rows, :] = total[rows, :] * factor
        counts.append(count)
    depth = len(colours[0][2])
    for s in range(depth - 1, -1, -1):
        moves = []
        for c, (_, _, plan) in enumerate(colours):
            axis, bit, halve, count = plan[s]
            if not halve:
                continue
            _, other = partner_of(axis, bit)
            rows = pl.ds(pl.multiple_of(trail[c][s], 8), count)
            copy = pltpu.make_async_remote_copy(
                src_ref=out_ref.at[rows],
                dst_ref=out_ref.at[rows],
                send_sem=back_send.at[c, s],
                recv_sem=back_recv.at[c, s],
                device_id={axis: other},
                device_id_type=pl.DeviceIdType.MESH,
            )
            copy.start()
            moves.append(copy)
        for copy in moves:
            copy.wait()


def reduce_weights(grads, axis_sizes, factor, chans):
    rows, lanes = grads.shape
    colours = colours_of(stages_of(axis_sizes), rows, chans)
    depth = len(colours[0][2])
    landing = sum(count for _, _, plan in colours for _, _, _, count in plan)
    sems = pltpu.SemaphoreType.DMA((len(colours), depth))
    return pl.pallas_call(
        functools.partial(reduce_kernel, colours, factor),
        out_shape=jax.ShapeDtypeStruct((rows, lanes), F32),
        in_specs=[VMEM],
        out_specs=VMEM,
        scratch_shapes=[
            pltpu.VMEM((rows, lanes), F32),
            pltpu.VMEM((landing, lanes), F32),
            sems,
            sems,
            sems,
            sems,
        ],
        compiler_params=pltpu.CompilerParams(collective_id=0, has_side_effects=True),
        name="reduce_weights",
    )(grads)


def shape_of(*dims, dtype=BF16):
    return jax.ShapeDtypeStruct(dims, dtype)


def body(
    axis_sizes,
    signal,
    cotangent,
    conv_weight,
    mix_weight,
    send_rows,
    send_mask,
    tile_vals,
    tile_row,
    tile_col,
    tile_mask,
    hub_owner,
    hub_rows,
):
    nodes, b_dev, steps, chans = signal.shape
    out_steps = steps - 1
    features = out_steps * chans
    n_dom, cap = send_rows.shape
    hub_per = hub_rows.shape[1]
    width = cap + hub_per
    slots = n_dom * width
    block = tile_vals.shape[1]
    all_tiles = (nodes + n_dom * cap + hub_rows.size) // block
    me = lax.axis_index("dom")

    sig = signal.reshape(nodes, steps * chans)
    cot = cotangent.reshape(nodes, features)

    mine = hub_owner == me
    own_hub = jnp.sum(jnp.where(mine[:, None], hub_rows + 1, 0), axis=0) - 1
    pick = jnp.concatenate(
        [
            jnp.where(send_mask == 1, send_rows, -1),
            jnp.broadcast_to(own_hub[None, :], (n_dom, hub_per)),
        ],
        axis=1,
    ).reshape(slots, 1)
    place = jnp.concatenate(
        [
            (
                jnp.arange(n_dom, dtype=jnp.int32)[:, None] * width
                + jnp.arange(cap, dtype=jnp.int32)[None, :]
            ).reshape(-1, 1),
            (
                hub_owner[:, None] * width + cap + jnp.arange(hub_per, dtype=jnp.int32)[None, :]
            ).reshape(-1, 1),
        ],
        axis=0,
    )

    own, far, send, hidden, tanh_filt, sig_gate, back_two, out_one = pl.pallas_call(
        pre_kernel,
        out_shape=(
            shape_of(nodes, nodes),
            shape_of(nodes, slots),
            shape_of(slots, nodes),
            shape_of(nodes, features),
            shape_of(nodes, features, dtype=F32),
            shape_of(nodes, features, dtype=F32),
            shape_of(nodes, features),
            shape_of(slots, 2 * features),
        ),
        in_specs=[SMEM] * 3 + [VMEM] * 7,
        out_specs=(VMEM,) * 8,
        scratch_shapes=[
            pltpu.VMEM((all_tiles, nodes, block), F32),
            pltpu.VMEM((2 * chans, 2 * chans), BF16),
        ],
        name="pre",
    )(tile_row, tile_col, tile_mask, sig, cot, conv_weight, mix_weight, tile_vals, pick, place)

    in_one = lax.all_to_all(out_one, "dom", split_axis=0, concat_axis=0, tiled=True)
    hop_one, back_one, out_two = pl.pallas_call(
        mid_kernel,
        out_shape=(
            shape_of(nodes, features),
            shape_of(nodes, features),
            shape_of(slots, 2 * features),
        ),
        in_specs=[VMEM] * 8,
        out_specs=(VMEM,) * 3,
        name="mid",
    )(own, far, send, hidden, back_two, cot, mix_weight, in_one)
    in_two = lax.all_to_all(out_two, "dom", split_axis=0, concat_axis=0, tiled=True)
    layer_out, signal_grad, grads = pl.pallas_call(
        post_kernel,
        out_shape=(
            shape_of(nodes, features),
            shape_of(nodes, steps * chans),
            shape_of(7 * chans, chans, dtype=F32),
        ),
        in_specs=[VMEM] * 13,
        out_specs=(VMEM,) * 3,
        scratch_shapes=[
            pltpu.VMEM((2 * chans, 2 * chans), BF16),
            pltpu.VMEM((nodes, chans), BF16),
            pltpu.VMEM((nodes, 2 * chans), BF16),
        ],
        name="post",
    )(
        own,
        far,
        send,
        hidden,
        hop_one,
        back_one,
        in_two,
        sig,
        cot,
        tanh_filt,
        sig_gate,
        conv_weight,
        mix_weight,
    )
    total_count = nodes * out_steps * b_dev
    for _, size in axis_sizes:
        total_count *= size
    reduced = reduce_weights(grads, axis_sizes, 1.0 / math.sqrt(total_count), chans)
    return (
        layer_out.reshape(nodes, b_dev, out_steps, chans),
        signal_grad.reshape(signal.shape),
        reduced[: 4 * chans].reshape(conv_weight.shape),
        reduced[4 * chans :].reshape(mix_weight.shape),
    )


def solution(mesh):
    placed = (
        P("dom", "batch", None, None),
        P("dom", "batch", None, None),
        P(),
        P(),
        P("dom", None),
        P("dom", None),
        P("dom", None, None),
        P("dom"),
        P("dom"),
        P("dom"),
        P(),
        P(),
    )
    axis_sizes = tuple((axis, mesh.shape[axis]) for axis in ("dom", "batch"))
    return jax.shard_map(
        functools.partial(body, axis_sizes),
        mesh=mesh,
        in_specs=placed,
        out_specs=(P("dom", "batch", None, None), P("dom", "batch", None, None), P(), P()),
        check_vma=False,
    )
```

time: 557 us -> 135 us (0.24); the launches traced: 550 us -> 135 us
  waiting for transfers between devices: 237 us -> 0 us
  matrix products: 83.2 us -> 0 us
  local copies, waits for them, and re-layouts: 94.4 us -> 13 us
  Pallas kernels: 0 us -> 67.2 us
  blocking collectives: 83.4 us -> 51 us
  starting transfers between devices: 21.9 us -> 0 us
  between operations: 14.6 us -> 0.69 us
  other arithmetic: 15.9 us -> 3.05 us
    psum x3 -> x0, waiting for transfers between devices: 237 us -> none  [the longest x1 127 us: body(): conv_total, mix_total = lax.psum((conv_part, mix_part), ('dom', 'batch'))]
    psum x2 -> x0, blocking collectives: 83.4 us -> none  [spread(): hubs = lax.psum(placed, 'dom').astype(jnp.bfloat16)]
    dot_general x33 -> x0, matrix products: 83.2 us -> none  [the longest x14 20.6 us: mm(): return jnp.dot(left, right, preferred_element_type=jnp.float32)]
    pallas_call x0 -> x4, Pallas kernels: none -> 67.2 us  [the longest x1 45.3 us: reduce_weights(): pl.pallas_call(functools.partial(reduce_kernel, colours, factor), out_sha...]
    all_to_all x0 -> x2, blocking collectives: none -> 51 us  [the longest x1 27.6 us: body(): lax.all_to_all(out_one, 'dom', split_axis=0, concat_axis=0, tiled=True)]
    dot_general x4 -> x0, local copies, waits for them, and re-layouts: 26.8 us -> none  [the longest x2 13.4 us: tile_back(): jnp.einsum('tji,tjf->tif', tile_block, chosen, preferred_element_type=jnp...]
    all_to_all x4 -> x0, starting transfers between devices: 21.3 us -> none  [the longest x2 11.1 us: gather_back(): lax.all_to_all(ext_grad[node_dev:node_dev + halo_count].astype(jnp.bfloat...]
    reshape x11 -> x3, local copies, waits for them, and re-layouts: 19.3 us -> 3.5 us  [the longest x1 1.56 us: body(): signal_grad.reshape(signal.shape)]
  transfers between devices with their start and end apart: 7 -> 0, of which waited for: 3 -> 0; matrix products, arithmetic and copies ran while one was open for 10% -> 0% of each run, Pallas kernels for 0% -> 0%
where the time goes in v1:
time: 135 us
  Pallas kernels  67.2 us (50%)
  blocking collectives  51 us (38%)
  local copies, waits for them, and re-layouts  13 us (10%)
  other arithmetic  3.05 us (2%)
    pallas_call x1, Pallas kernels, reduce_weights(): pl.pallas_call(functools.partial(reduce_kernel, colours, factor), out_sha...  45.3 us
    all_to_all x1, blocking collectives, body(): lax.all_to_all(out_one, 'dom', split_axis=0, concat_axis=0, tiled=True)  27.6 us
    all_to_all x1, blocking collectives, body(): lax.all_to_all(out_two, 'dom', split_axis=0, concat_axis=0, tiled=True)  23.5 us
    pallas_call x1, Pallas kernels, body(): pl.pallas_call(post_kernel, out_shape=(shape_of(nodes, features), shape_o...  10.2 us
    pallas_call x1, Pallas kernels, body(): pl.pallas_call(pre_kernel, out_shape=(shape_of(nodes, nodes), shape_of(no...  6.31 us
    pallas_call x1, Pallas kernels, body(): pl.pallas_call(mid_kernel, out_shape=(shape_of(nodes, features), shape_of...  5.37 us
    unnamed x9, local copies, waits for them, and re-layouts  3.77 us

profile of v1, /device:TPU:0, one launch (start us, length us, event | category | flops | bytes accessed | tf_op | source)
XLA Modules:
  0.0 135.0 jit_solution(363089490939775273)
XLA Ops:
  0.6 0.0 copy-start
  0.7 0.7 multiply_add_fusion
  1.4 0.7 broadcast_compare_fusion
  2.1 0.8 select_reduce_fusion
  2.8 0.1 iota_add_fusion.1
  2.9 0.1 add.62
  3.0 0.1 iota_add_fusion
  3.1 0.1 add.67
  3.1 0.1 pad.3.clone
  3.2 0.7 compare_select_fusion
  3.9 0.8 reshape.98.pick_ref
  4.7 0.8 copy.34.place_ref
  5.5 1.4 %copy.31 = bf16[512,1,3,256]{0,3,2,1:T(8,128)(2,1)S(1)} copy(bf16[512,1,3,256]{3,0,2,1:T(8,128)(2,1)} %param.13) | data formatting | bytes 1572864 | tf_op args[1]
  6.9 1.2 copy.32.cot_ref
  8.1 0.0 copy-done
  8.1 1.2 copy.40
  9.3 6.3 %pre.1 = (bf16[512,512]{1,0:T(8,128)(2,1)}, bf16[512,256]{1,0:T(8,128)(2,1)}, bf16[256,512]{1,0:T(8,128)(2,1)}, bf16[512,768]{1,0:T(8,128)(2,1)}, f32[512,768]{1...) custom-call(s32[16]{0:T(128)} %row_ref.1, s32[16]{0:T(128)} %col_ref.1, ...), custom_call_target="tpu_custom_call" | custom-call | tf_op jit(solution)/shard_map/pre/pallas_call | solution.py:394
  15.6 27.6 %all_to_all.22 = bf16[8,32,1536]{2,1,0:T(8,128)(2,1)} all-to-all(bf16[8,32,1536]{2,1,0:T(8,128)(2,1)} %bitcast.22), channel_id=1, replica_groups=mesh['dom'=8,'batch'=4] {'dom'}, dimensions={0} | all-to-all | bytes 1572864 | tf_op jit(solution)/shard_map/all_to_all | solution.py:415
  43.2 5.4 %mid.1 = (bf16[512,768]{1,0:T(8,128)(2,1)}, bf16[512,768]{1,0:T(8,128)(2,1)}, bf16[256,1536]{1,0:T(8,128)(2,1)}) custom-call(bf16[512,512]{1,0:T(8,128)(2,1)} %get-tuple-element.18.own_ref, bf16[512,256]{1,0:T(8,128)(2,1)} %get-tuple-element.19.far_ref, bf16[256,512]{1,0:T(8,128)(2,1)} %get-tuple-element.20.send_ref, ...), custom_call_target="tpu_custom_call" | custom-call | tf_op jit(solution)/shard_map/mid/pallas_call | solution.py:416
  48.5 23.5 %all_to_all.23 = bf16[8,32,1536]{2,1,0:T(8,128)(2,1)} all-to-all(bf16[8,32,1536]{2,1,0:T(8,128)(2,1)} %bitcast.23), channel_id=1, replica_groups=mesh['dom'=8,'batch'=4] {'dom'}, dimensions={0} | all-to-all | bytes 1572864 | tf_op jit(solution)/shard_map/all_to_all | solution.py:427
  72.0 10.2 %post.1 = (bf16[512,768]{1,0:T(8,128)(2,1)}, bf16[512,1024]{1,0:T(8,128)(2,1)}, f32[1792,256]{1,0:T(8,128)}) custom-call(bf16[512,512]{1,0:T(8,128)(2,1)} %get-tuple-element.18.own_ref, bf16[512,256]{1,0:T(8,128)(2,1)} %get-tuple-element.19.far_ref, bf16[256,512]{1,0:T(8,128)(2,1)} %get-tuple-element.20.send_ref, ...), custom_call_target="tpu_custom_call" | custom-call | tf_op jit(solution)/shard_map/post/pallas_call | solution.py:428
  82.2 45.3 %reduce_weights.1 = f32[1792,256]{1,0:T(8,128)} custom-call(f32[1792,256]{1,0:T(8,128)} %get-tuple-element.31.grads_ref), custom_call_target="tpu_custom_call" | custom-call | tf_op jit(solution)/shard_map/reduce_weights/pallas_call | solution.py:321
  127.6 0.0 copy-start.2
  127.6 2.1 %slice.7 = f32[768,256]{1,0:T(8,128)} slice(f32[1792,256]{1,0:T(8,128)} %reduce_weights.1), slice={[1024:1792], [0:256]} | slice | bytes 1572864 | tf_op jit(solution)/shard_map/slice | solution.py:466
  129.7 2.3 %slice.6 = f32[1024,256]{1,0:T(8,128)} slice(f32[1792,256]{1,0:T(8,128)} %reduce_weights.1), slice={[0:1024], [0:256]} | slice | bytes 2097152 | tf_op jit(solution)/shard_map/slice | solution.py:465
  132.0 0.0 copy-start.1
  132.0 0.0 copy-done.2
  132.0 0.3 copy.37
  132.3 1.2 copy.38
  133.4 0.0 copy-done.1
  133.4 1.6 %reshape.95 = bf16[512,1,4,256]{3,2,0,1:T(4,128)(2,1)} reshape(bf16[512,1024]{1,0:T(8,128)(2,1)S(1)} %copy-done.1) | data formatting | bytes 2097152 | tf_op jit(solution)/shard_map/reshape | solution.py:464
  (4 shorter events, 0.0 us)
Async XLA Ops:
  0.6 7.5 %copy-start = (bf16[512,1,4,256]{3,2,1,0:T(4,128)(2,1)S(1)}, bf16[512,1,4,256]{3,2,1,0:T(4,128)(2,1)}, u32[]{:S(2)}) copy-start(bf16[512,1,4,256]{3,2,1,0:T(4,128)(2,1)} %param.12) | copy-start | bytes 3145732
  127.6 4.4 %copy-start.2 = (bf16[512,768]{1,0:T(8,128)(2,1)S(1)}, bf16[512,768]{1,0:T(8,128)(2,1)}, u32[]{:S(2)}) copy-start(bf16[512,768]{1,0:T(8,128)(2,1)} %get-tuple-element.29) | copy-start | bytes 2359300
  132.0 1.4 %copy-start.1 = (bf16[512,1024]{1,0:T(8,128)(2,1)S(1)}, bf16[512,1024]{1,0:T(8,128)(2,1)}, u32[]{:S(2)}) copy-start(bf16[512,1024]{1,0:T(8,128)(2,1)} %get-tuple-element.30) | copy-start | bytes 3145732

commit v2 on v1

--- a/solution.py
+++ b/solution.py
@@ -3,6 +3,7 @@
 
 import jax
 import jax.numpy as jnp
+import numpy as np
 from jax import lax
 from jax.experimental import pallas as pl
 from jax.experimental.pallas import tpu as pltpu
@@ -44,8 +45,13 @@
     conv_ref,
     mix_ref,
     tile_ref,
-    pick_ref,
-    place_ref,
+    owner_ref,
+    rows_ref,
+    flag_ref,
+    hubs_ref,
+    expand_ref,
+    lane_ref,
+    halo_ref,
     own_ref,
     far_ref,
     send_ref,
@@ -55,6 +61,7 @@
     back_ref,
     out_ref,
     dense_ref,
+    place_ref,
     taps_ref,
 ):
     nodes = own_ref.shape[0]
@@ -75,16 +82,45 @@
     for c in range(own_tiles):
         own_ref[:, c * block : (c + 1) * block] = dense_ref[c].astype(BF16)
     slots = send_ref.shape[0]
-    place = (
-        place_ref[...] == lax.broadcasted_iota(jnp.int32, (place_ref.shape[0], slots), 1)
-    ).astype(BF16)
-    far = nn(dense_ref[own_tiles].astype(BF16), place[:block])
+    cap = rows_ref.shape[1]
+    groups, hub_per = hubs_ref.shape
+    width = cap + hub_per
+    halo = halo_ref.shape[0]
+    place_ref[:halo, :] = halo_ref[...]
+    slot = lax.broadcasted_iota(jnp.int32, (hub_per, slots), 1)
+    entry = lax.broadcasted_iota(jnp.int32, (hub_per, slots), 0) + cap
+    me = lax.axis_index("dom")
+    hub = jnp.zeros((1, hub_per), F32)
+    for o in range(groups):
+        at = halo + o * hub_per
+        owner = owner_ref[o]
+        place_ref[at : at + hub_per, :] = jnp.where(slot == entry + owner * width, 1.0, 0.0).astype(
+            BF16
+        )
+        owned = (owner == me).astype(F32)
+        hub += owned * (hubs_ref[o : o + 1, :].astype(F32) + 1.0)
+    far = nn(dense_ref[own_tiles].astype(BF16), place_ref[:block, :])
     for c in range(own_tiles + 1, all_tiles):
         at = (c - own_tiles) * block
-        far += nn(dense_ref[c].astype(BF16), place[at : at + block])
+        far += nn(dense_ref[c].astype(BF16), place_ref[at : at + block, :])
     far_ref[...] = far.astype(BF16)
-    send_ref[...] = (
-        pick_ref[...] == lax.broadcasted_iota(jnp.int32, (slots, nodes), 1)
+    chosen = jnp.where(flag_ref[...] == 1, rows_ref[...].astype(F32) + 1.0, 0.0)
+    spread = jnp.dot(
+        expand_ref[...], chosen, precision=lax.Precision.HIGHEST, preferred_element_type=F32
+    )
+    lane = lane_ref[...]
+    from_halo = jnp.where(
+        lax.broadcasted_iota(jnp.int32, (slots, cap), 1) == lane, spread, 0.0
+    )
+    from_hub = jnp.where(
+        lax.broadcasted_iota(jnp.int32, (slots, hub_per), 1) + cap == lane,
+        jnp.broadcast_to(hub, (slots, hub_per)),
+        0.0,
+    )
+    pick = jnp.sum(from_halo, axis=1, keepdims=True) + jnp.sum(from_hub, axis=1, keepdims=True)
+    pick = (pick + 0.5).astype(jnp.int32) - 1
+    send_ref[...] = jnp.where(
+        pick == lax.broadcasted_iota(jnp.int32, (slots, nodes), 1), 1.0, 0.0
     ).astype(BF16)
 
     fill_taps(conv_ref, taps_ref)
@@ -96,7 +132,7 @@
         tanh_ref[:, at] = tanh_filt
         gate_ref[:, at] = sig_gate
         hidden_ref[:, at] = (tanh_filt * sig_gate).astype(BF16)
-        back_ref[:, at] = nt(cot_ref[:, at], mix_ref[2]).astype(BF16)
+        back_ref[:, at] = nt(cot_ref[t], mix_ref[2]).astype(BF16)
     out_ref[:, :features] = nn(send_ref[...], hidden_ref[...]).astype(BF16)
     out_ref[:, features:] = tn(far_ref[...], back_ref[...]).astype(BF16)
 
@@ -123,7 +159,7 @@
             nn(own_ref[...], hidden_ref[:, at]) + nn(far_ref[...], in_ref[:, at])
         ).astype(BF16)
         next_ref[:, at] = (
-            nt(cot_ref[:, at], mix_ref[1])
+            nt(cot_ref[t], mix_ref[1])
             + tn(own_ref[...], back_ref[:, at])
             + tn(send_ref[...], in_ref[:, late])
         ).astype(BF16)
@@ -160,11 +196,11 @@
         at = slice(t * chans, (t + 1) * chans)
         after = slice((t + 1) * chans, (t + 2) * chans)
         late = slice(features + t * chans, features + (t + 1) * chans)
-        cot = cot_ref[:, at]
+        cot = cot_ref[t]
         last_ref[...] = (
             nn(own_ref[...], hop_ref[:, at]) + nn(far_ref[...], in_ref[:, at])
         ).astype(BF16)
-        layer_ref[:, at] = (
+        layer_ref[t] = (
             sig_ref[:, after].astype(F32)
             + nn(hidden_ref[:, at], mix_ref[0])
             + nn(hop_ref[:, at], mix_ref[1])
@@ -226,7 +262,7 @@
     for order, share in zip(orders, shares):
         plan, count = [], share * chans
         for axis, bit in order:
-            halve = (count // 2) % 8 == 0
+            halve = (count // 2) % 16 == 0
             plan.append((axis, bit, halve, count // 2 if halve else count))
             if halve:
                 count //= 2
@@ -241,8 +277,32 @@
     return mine, index + bit - 2 * bit * mine
 
 
+def narrow(stage):
+    return stage in (1, 2)
+
+
+def landing_rows(colours, wanted):
+    return sum(
+        count
+        for _, _, plan in colours
+        for stage, (_, _, _, count) in enumerate(plan)
+        if narrow(stage) == wanted
+    )
+
+
 def reduce_kernel(
-    colours, factor, grads_ref, out_ref, total, landing, send_sem, recv_sem, back_send, back_recv
+    colours,
+    factor,
+    grads_ref,
+    out_ref,
+    total,
+    wide,
+    landed,
+    leaving,
+    send_sem,
+    recv_sem,
+    back_send,
+    back_recv,
 ):
     barrier = pltpu.get_barrier_semaphore()
     peers = sorted({(axis, bit) for axis, bit, _, _ in colours[0][2]})
@@ -255,41 +315,43 @@
 
     starts = [base for base, _, _ in colours]
     trail = [[] for _ in colours]
-    landed = 0
-    for s in range(len(colours[0][2])):
+    used = {True: 0, False: 0}
+    depth = len(colours[0][2])
+    for s in range(depth):
         moves = []
+        small = narrow(s)
+        landing = landed if small else wide
         for c, (_, _, plan) in enumerate(colours):
             axis, bit, halve, count = plan[s]
             mine, other = partner_of(axis, bit)
             source = grads_ref if s == 0 else total
             keep = starts[c] + mine * count if halve else starts[c]
             give = starts[c] + (1 - mine) * count if halve else starts[c]
-            give_rows = pl.ds(pl.multiple_of(give, 8), count)
-            keep_rows = pl.ds(pl.multiple_of(keep, 8), count)
+            give_rows = pl.ds(pl.multiple_of(give, 16), count)
+            keep_rows = pl.ds(pl.multiple_of(keep, 16), count)
+            spot = pl.ds(used[small], count)
+            if small:
+                leaving[spot, :] = source[give_rows, :].astype(BF16)
             copy = pltpu.make_async_remote_copy(
-                src_ref=source.at[give_rows],
-                dst_ref=landing.at[pl.ds(landed, count)],
+                src_ref=leaving.at[spot] if small else source.at[give_rows],
+                dst_ref=landing.at[spot],
                 send_sem=send_sem.at[c, s],
                 recv_sem=recv_sem.at[c, s],
                 device_id={axis: other},
                 device_id_type=pl.DeviceIdType.MESH,
             )
             copy.start()
-            moves.append((copy, source, keep_rows, landed, count))
-            landed += count
+            moves.append((copy, source, keep_rows, spot))
+            used[small] += count
             trail[c].append(keep)
             starts[c] = keep
-        for copy, source, keep_rows, at, count in moves:
+        for copy, source, keep_rows, spot in moves:
             copy.wait()
-            total[keep_rows, :] = source[keep_rows, :] + landing[at : at + count, :]
-
-    counts = []
+            total[keep_rows, :] = source[keep_rows, :] + landing[spot, :].astype(F32)
+
     for c, (_, _, plan) in enumerate(colours):
-        count = plan[-1][3]
-        rows = pl.ds(pl.multiple_of(starts[c], 8), count)
-        out_ref[rows, :] = total[rows, :] * factor
-        counts.append(count)
-    depth = len(colours[0][2])
+        rows = pl.ds(pl.multiple_of(starts[c], 16), plan[-1][3])
+        out_ref[rows, :] = (total[rows, :] * factor).astype(BF16)
     for s in range(depth - 1, -1, -1):
         moves = []
         for c, (_, _, plan) in enumerate(colours):
@@ -297,7 +359,7 @@
             if not halve:
                 continue
             _, other = partner_of(axis, bit)
-            rows = pl.ds(pl.multiple_of(trail[c][s], 8), count)
+            rows = pl.ds(pl.multiple_of(trail[c][s], 16), count)
             copy = pltpu.make_async_remote_copy(
                 src_ref=out_ref.at[rows],
                 dst_ref=out_ref.at[rows],
@@ -315,17 +377,18 @@
 def reduce_weights(grads, axis_sizes, factor, chans):
     rows, lanes = grads.shape
     colours = colours_of(stages_of(axis_sizes), rows, chans)
-    depth = len(colours[0][2])
-    landing = sum(count for _, _, plan in colours for _, _, _, count in plan)
-    sems = pltpu.SemaphoreType.DMA((len(colours), depth))
+    sems = pltpu.SemaphoreType.DMA((len(colours), len(colours[0][2])))
+    slim = landing_rows(colours, True)
     return pl.pallas_call(
         functools.partial(reduce_kernel, colours, factor),
-        out_shape=jax.ShapeDtypeStruct((rows, lanes), F32),
+        out_shape=jax.ShapeDtypeStruct((rows, lanes), BF16),
         in_specs=[VMEM],
         out_specs=VMEM,
         scratch_shapes=[
             pltpu.VMEM((rows, lanes), F32),
-            pltpu.VMEM((landing, lanes), F32),
+            pltpu.VMEM((landing_rows(colours, False), lanes), F32),
+            pltpu.VMEM((slim, lanes), BF16),
+            pltpu.VMEM((slim, lanes), BF16),
             sems,
             sems,
             sems,
@@ -364,31 +427,16 @@
     slots = n_dom * width
     block = tile_vals.shape[1]
     all_tiles = (nodes + n_dom * cap + hub_rows.size) // block
-    me = lax.axis_index("dom")
 
     sig = signal.reshape(nodes, steps * chans)
-    cot = cotangent.reshape(nodes, features)
-
-    mine = hub_owner == me
-    own_hub = jnp.sum(jnp.where(mine[:, None], hub_rows + 1, 0), axis=0) - 1
-    pick = jnp.concatenate(
-        [
-            jnp.where(send_mask == 1, send_rows, -1),
-            jnp.broadcast_to(own_hub[None, :], (n_dom, hub_per)),
-        ],
-        axis=1,
-    ).reshape(slots, 1)
-    place = jnp.concatenate(
-        [
-            (
-                jnp.arange(n_dom, dtype=jnp.int32)[:, None] * width
-                + jnp.arange(cap, dtype=jnp.int32)[None, :]
-            ).reshape(-1, 1),
-            (
-                hub_owner[:, None] * width + cap + jnp.arange(hub_per, dtype=jnp.int32)[None, :]
-            ).reshape(-1, 1),
-        ],
-        axis=0,
+    cot = jnp.transpose(cotangent.reshape(nodes, out_steps, chans), (1, 0, 2))
+
+    slot = np.arange(slots)
+    expand = (slot[:, None] // width == np.arange(n_dom)[None, :]).astype(np.float32)
+    lane = (slot % width).astype(np.int32)[:, None]
+    entry = np.arange(n_dom * cap)
+    halo = jnp.asarray(
+        (entry // cap * width + entry % cap)[:, None] == slot[None, :], dtype=BF16
     )
 
     own, far, send, hidden, tanh_filt, sig_gate, back_two, out_one = pl.pallas_call(
@@ -403,14 +451,31 @@
             shape_of(nodes, features),
             shape_of(slots, 2 * features),
         ),
-        in_specs=[SMEM] * 3 + [VMEM] * 7,
+        in_specs=[SMEM] * 3 + [VMEM] * 5 + [SMEM] + [VMEM] * 6,
         out_specs=(VMEM,) * 8,
         scratch_shapes=[
             pltpu.VMEM((all_tiles, nodes, block), F32),
+            pltpu.VMEM((n_dom * cap + hub_rows.size, slots), BF16),
             pltpu.VMEM((2 * chans, 2 * chans), BF16),
         ],
         name="pre",
-    )(tile_row, tile_col, tile_mask, sig, cot, conv_weight, mix_weight, tile_vals, pick, place)
+    )(
+        tile_row,
+        tile_col,
+        tile_mask,
+        sig,
+        cot,
+        conv_weight,
+        mix_weight,
+        tile_vals,
+        hub_owner,
+        send_rows,
+        send_mask,
+        hub_rows,
+        expand,
+        lane,
+        halo,
+    )
 
     in_one = lax.all_to_all(out_one, "dom", split_axis=0, concat_axis=0, tiled=True)
     hop_one, back_one, out_two = pl.pallas_call(
@@ -428,7 +493,7 @@
     layer_out, signal_grad, grads = pl.pallas_call(
         post_kernel,
         out_shape=(
-            shape_of(nodes, features),
+            shape_of(out_steps, nodes, chans),
             shape_of(nodes, steps * chans),
             shape_of(7 * chans, chans, dtype=F32),
         ),
@@ -460,10 +525,10 @@
         total_count *= size
     reduced = reduce_weights(grads, axis_sizes, 1.0 / math.sqrt(total_count), chans)
     return (
-        layer_out.reshape(nodes, b_dev, out_steps, chans),
+        jnp.transpose(layer_out, (1, 0, 2)).reshape(nodes, b_dev, out_steps, chans),
         signal_grad.reshape(signal.shape),
-        reduced[: 4 * chans].reshape(conv_weight.shape),
-        reduced[4 * chans :].reshape(mix_weight.shape),
+        reduced[: 4 * chans].astype(F32).reshape(conv_weight.shape),
+        reduced[4 * chans :].astype(F32).reshape(mix_weight.shape),
     )
 
 

time: 135 us -> 119 us (0.88)
  local copies, waits for them, and re-layouts: 13 us -> 4.97 us
  Pallas kernels: 67.2 us -> 59.8 us
    pallas_call x1, Pallas kernels: 45.3 us -> 38 us  [reduce_weights(): pl.pallas_call(functools.partial(reduce_kernel, colours, factor), out_sha...]
    slice x2 -> x4, local copies, waits for them, and re-layouts: 4.4 us -> 0.97 us  [the longest x2 0.97 us: body(): reduced[4 * chans:].astype(F32).reshape(mix_weight.shape)]
    reshape x0 -> x2, other arithmetic: none -> 2 us  [the longest x1 1.06 us: body(): reduced[:4 * chans].astype(F32).reshape(conv_weight.shape)]
    reshape x2 -> x0, local copies, waits for them, and re-layouts: 1.94 us -> none  [the longest x1 1.15 us: body(): cot = cotangent.reshape(nodes, features)]
    unnamed x9 -> x3, local copies, waits for them, and re-layouts: 3.77 us -> 2.43 us
where the time goes in v2:
time: 119 us
  Pallas kernels  59.8 us (50%)
  blocking collectives  51.1 us (43%)
  local copies, waits for them, and re-layouts  4.97 us (4%)
  other arithmetic  2 us (2%)
    pallas_call x1, Pallas kernels, reduce_weights(): pl.pallas_call(functools.partial(reduce_kernel, colours, factor), out_sha...  38 us
    all_to_all x1, blocking collectives, body(): lax.all_to_all(out_one, 'dom', split_axis=0, concat_axis=0, tiled=True)  27.6 us
    all_to_all x1, blocking collectives, body(): lax.all_to_all(out_two, 'dom', split_axis=0, concat_axis=0, tiled=True)  23.5 us
    pallas_call x1, Pallas kernels, body(): pl.pallas_call(post_kernel, out_shape=(shape_of(out_steps, nodes, chans),...  10.2 us
    pallas_call x1, Pallas kernels, body(): pl.pallas_call(pre_kernel, out_shape=(shape_of(nodes, nodes), shape_of(no...  6.32 us
    pallas_call x1, Pallas kernels, body(): pl.pallas_call(mid_kernel, out_shape=(shape_of(nodes, features), shape_of...  5.31 us
    unnamed x3, local copies, waits for them, and re-layouts  2.43 us

profile of v2, /device:TPU:0, one launch (start us, length us, event | category | flops | bytes accessed | tf_op | source)
XLA Modules:
  0.0 118.5 jit_solution(3319020616220828097)
XLA Ops:
  0.6 2.4 %copy.20 = bf16[64,8,4,256]{3,1,2,0:T(8,128)(2,1)} copy(bf16[64,8,4,256]{3,2,1,0:T(4,128)(2,1)} %bitcast.27) | data formatting | bytes 2097152
  3.1 6.3 %pre.1 = (bf16[512,512]{1,0:T(8,128)(2,1)}, bf16[512,256]{1,0:T(8,128)(2,1)}, bf16[256,512]{1,0:T(8,128)(2,1)}, bf16[512,768]{1,0:T(8,128)(2,1)}, f32[512,768]{1...) custom-call(s32[16]{0:T(128)} %row_ref.1, s32[16]{0:T(128)} %col_ref.1, ...), custom_call_target="tpu_custom_call" | custom-call | tf_op jit(solution)/shard_map/pre/pallas_call | solution.py:442
  9.4 27.6 %all_to_all.22 = bf16[8,32,1536]{2,1,0:T(8,128)(2,1)} all-to-all(bf16[8,32,1536]{2,1,0:T(8,128)(2,1)} %bitcast.29), channel_id=1, replica_groups=mesh['dom'=8,'batch'=4] {'dom'}, dimensions={0} | all-to-all | bytes 1572864 | tf_op jit(solution)/shard_map/all_to_all | solution.py:480
  36.9 5.3 %mid.1 = (bf16[512,768]{1,0:T(8,128)(2,1)}, bf16[512,768]{1,0:T(8,128)(2,1)}, bf16[256,1536]{1,0:T(8,128)(2,1)}) custom-call(bf16[512,512]{1,0:T(8,128)(2,1)} %get-tuple-element.18.own_ref, bf16[512,256]{1,0:T(8,128)(2,1)} %get-tuple-element.19.far_ref, bf16[256,512]{1,0:T(8,128)(2,1)} %get-tuple-element.20.send_ref, ...), custom_call_target="tpu_custom_call" | custom-call | tf_op jit(solution)/shard_map/mid/pallas_call | solution.py:481
  42.3 23.5 %all_to_all.23 = bf16[8,32,1536]{2,1,0:T(8,128)(2,1)} all-to-all(bf16[8,32,1536]{2,1,0:T(8,128)(2,1)} %bitcast.30), channel_id=1, replica_groups=mesh['dom'=8,'batch'=4] {'dom'}, dimensions={0} | all-to-all | bytes 1572864 | tf_op jit(solution)/shard_map/all_to_all | solution.py:492
  65.7 10.2 %post.1 = (bf16[3,512,256]{2,1,0:T(8,128)(2,1)}, bf16[512,1024]{1,0:T(8,128)(2,1)}, f32[1792,256]{1,0:T(8,128)}) custom-call(bf16[512,512]{1,0:T(8,128)(2,1)} %get-tuple-element.18.own_ref, bf16[512,256]{1,0:T(8,128)(2,1)} %get-tuple-element.19.far_ref, bf16[256,512]{1,0:T(8,128)(2,1)} %get-tuple-element.20.send_ref, ...), custom_call_target="tpu_custom_call" | custom-call | tf_op jit(solution)/shard_map/post/pallas_call | solution.py:493
  76.0 38.0 %reduce_weights.1 = bf16[1792,256]{1,0:T(8,128)(2,1)} custom-call(f32[1792,256]{1,0:T(8,128)} %get-tuple-element.31.grads_ref), custom_call_target="tpu_custom_call" | custom-call | tf_op jit(solution)/shard_map/reduce_weights/pallas_call | solution.py:382
  113.9 0.0 slice-start
  113.9 0.0 slice-start.1
  113.9 0.0 copy-start
  114.0 1.0 slice-done
  114.9 0.9 convert.3
  115.9 0.0 slice-done.1
  115.9 1.1 convert.2
  116.9 0.0 copy-done
  116.9 1.6 %reshape.39 = bf16[512,1,4,256]{3,2,0,1:T(4,128)(2,1)} reshape(bf16[512,1024]{1,0:T(8,128)(2,1)S(1)} %copy-done) | data formatting | bytes 2097152 | tf_op jit(solution)/shard_map/reshape | solution.py:529
Async XLA Ops:
  113.9 1.0 slice-start
  113.9 1.9 %slice-start.1 = ((bf16[1792,256]{1,0:T(8,128)(2,1)}), bf16[1024,256]{1,0:T(8,128)(2,1)S(1)}, s32[]{:S(2)}) async-start(bf16[1792,256]{1,0:T(8,128)(2,1)} %reduce_weights.1), calls=%async_computation.3 | async-start | bytes 1048576 | tf_op jit(solution)/shard_map/slice | solution.py:530
  113.9 3.0 %copy-start = (bf16[512,1024]{1,0:T(8,128)(2,1)S(1)}, bf16[512,1024]{1,0:T(8,128)(2,1)}, u32[]{:S(2)}) copy-start(bf16[512,1024]{1,0:T(8,128)(2,1)} %get-tuple-element.30) | copy-start | bytes 3145732

commit v3 on v2

--- a/solution.py
+++ b/solution.py
@@ -84,7 +84,7 @@
     slots = send_ref.shape[0]
     cap = rows_ref.shape[1]
     groups, hub_per = hubs_ref.shape
-    width = cap + hub_per
+    width = slots // expand_ref.shape[1]
     halo = halo_ref.shape[0]
     place_ref[:halo, :] = halo_ref[...]
     slot = lax.broadcasted_iota(jnp.int32, (hub_per, slots), 1)
@@ -137,7 +137,46 @@
     out_ref[:, features:] = tn(far_ref[...], back_ref[...]).astype(BF16)
 
 
+def rows_of(index, width):
+    return pl.ds(pl.multiple_of(index * width, 16), width)
+
+
+def exchange(devices, out_ref, in_ref, send_sem, recv_sem):
+    slots, lanes = out_ref.shape
+    width = slots // devices
+    half = lanes // 2
+    me = lax.axis_index("dom")
+    barrier = pltpu.get_barrier_semaphore()
+    for d in range(1, devices):
+        pl.semaphore_signal(
+            barrier,
+            inc=1,
+            device_id={"dom": lax.rem(me + d, devices)},
+            device_id_type=pl.DeviceIdType.MESH,
+        )
+    pl.semaphore_wait(barrier, devices - 1)
+    groups = []
+    for k, span in enumerate((slice(half, lanes), slice(0, half))):
+        copies = []
+        for d in range(1, devices):
+            other = lax.rem(me + d, devices)
+            copy = pltpu.make_async_remote_copy(
+                src_ref=out_ref.at[rows_of(other, width), span],
+                dst_ref=in_ref.at[rows_of(me, width), span],
+                send_sem=send_sem.at[k, d - 1],
+                recv_sem=recv_sem.at[k, d - 1],
+                device_id={"dom": other},
+                device_id_type=pl.DeviceIdType.MESH,
+            )
+            copy.start()
+            copies.append(copy)
+        groups.append(copies)
+    in_ref[rows_of(me, width), :] = out_ref[rows_of(me, width), :]
+    return groups
+
+
 def mid_kernel(
+    devices,
     own_ref,
     far_ref,
     send_ref,
@@ -145,36 +184,44 @@
     back_ref,
     cot_ref,
     mix_ref,
-    in_ref,
+    leave_ref,
     hop_ref,
     next_ref,
     out_ref,
+    in_ref,
+    hop_sum,
+    next_sum,
+    send_sem,
+    recv_sem,
 ):
     features = hidden_ref.shape[1]
     chans = mix_ref.shape[1]
-    for t in range(features // chans):
-        at = slice(t * chans, (t + 1) * chans)
-        late = slice(features + t * chans, features + (t + 1) * chans)
-        hop_ref[:, at] = (
-            nn(own_ref[...], hidden_ref[:, at]) + nn(far_ref[...], in_ref[:, at])
-        ).astype(BF16)
-        next_ref[:, at] = (
-            nt(cot_ref[t], mix_ref[1])
-            + tn(own_ref[...], back_ref[:, at])
-            + tn(send_ref[...], in_ref[:, late])
-        ).astype(BF16)
+    spans = [slice(t * chans, (t + 1) * chans) for t in range(features // chans)]
+    late, early = exchange(devices, leave_ref, in_ref, send_sem, recv_sem)
+    for t, at in enumerate(spans):
+        next_sum[:, at] = nt(cot_ref[t], mix_ref[1]) + tn(own_ref[...], back_ref[:, at])
+        hop_sum[:, at] = nn(own_ref[...], hidden_ref[:, at])
+    for copy in late:
+        copy.wait_recv()
+    next_ref[...] = (next_sum[...] + tn(send_ref[...], in_ref[:, features:])).astype(BF16)
+    out_ref[:, features:] = tn(far_ref[...], next_ref[...]).astype(BF16)
+    for copy in early:
+        copy.wait_recv()
+    hop_ref[...] = (hop_sum[...] + nn(far_ref[...], in_ref[:, :features])).astype(BF16)
     out_ref[:, :features] = nn(send_ref[...], hop_ref[...]).astype(BF16)
-    out_ref[:, features:] = tn(far_ref[...], next_ref[...]).astype(BF16)
+    for copy in late + early:
+        copy.wait_send()
 
 
 def post_kernel(
+    devices,
     own_ref,
     far_ref,
     send_ref,
     hidden_ref,
     hop_ref,
     back_ref,
-    in_ref,
+    leave_ref,
     sig_ref,
     cot_ref,
     tanh_ref,
@@ -184,36 +231,43 @@
     layer_ref,
     grad_ref,
     weight_ref,
+    in_ref,
+    hop_sum,
+    layer_sum,
+    hidden_sum,
     taps_ref,
     last_ref,
     held_ref,
+    send_sem,
+    recv_sem,
 ):
     features = hidden_ref.shape[1]
     chans = mix_ref.shape[1]
-    steps = features // chans
+    spans = [slice(t * chans, (t + 1) * chans) for t in range(features // chans)]
+    late, early = exchange(devices, leave_ref, in_ref, send_sem, recv_sem)
+
+    def add_weight(spot, part, first):
+        place = slice(spot * chans, (spot + 1) * chans)
+        weight_ref[place, :] = part if first else weight_ref[place, :] + part
+
     fill_taps(conv_ref, taps_ref)
-    for t in range(steps):
-        at = slice(t * chans, (t + 1) * chans)
-        after = slice((t + 1) * chans, (t + 2) * chans)
-        late = slice(features + t * chans, features + (t + 1) * chans)
-        cot = cot_ref[t]
-        last_ref[...] = (
-            nn(own_ref[...], hop_ref[:, at]) + nn(far_ref[...], in_ref[:, at])
-        ).astype(BF16)
-        layer_ref[t] = (
-            sig_ref[:, after].astype(F32)
+    for t, at in enumerate(spans):
+        hidden_sum[:, at] = nt(cot_ref[t], mix_ref[0]) + tn(own_ref[...], back_ref[:, at])
+        hop_sum[:, at] = nn(own_ref[...], hop_ref[:, at])
+        layer_sum[:, at] = (
+            sig_ref[:, (t + 1) * chans : (t + 2) * chans].astype(F32)
             + nn(hidden_ref[:, at], mix_ref[0])
             + nn(hop_ref[:, at], mix_ref[1])
-            + nn(last_ref[...], mix_ref[2])
-        ).astype(BF16)
-        for k, source in enumerate((hidden_ref[:, at], hop_ref[:, at], last_ref[...])):
-            part = tn(source, cot)
-            place = slice((4 + k) * chans, (5 + k) * chans)
-            weight_ref[place, :] = part if t == 0 else weight_ref[place, :] + part
-        grad_hidden = (
-            nt(cot, mix_ref[0])
-            + tn(own_ref[...], back_ref[:, at])
-            + tn(send_ref[...], in_ref[:, late])
+        )
+        add_weight(4, tn(hidden_ref[:, at], cot_ref[t]), t == 0)
+        add_weight(5, tn(hop_ref[:, at], cot_ref[t]), t == 0)
+
+    for copy in late:
+        copy.wait_recv()
+    for t, at in enumerate(spans):
+        cot = cot_ref[t]
+        grad_hidden = hidden_sum[:, at] + tn(
+            send_ref[...], in_ref[:, features + t * chans : features + (t + 1) * chans]
         )
         tanh_filt = tanh_ref[:, at]
         sig_gate = gate_ref[:, at]
@@ -225,16 +279,23 @@
         for kind in range(2):
             for tap in range(2):
                 part = outer[tap * chans : (tap + 1) * chans, kind * chans : (kind + 1) * chans]
-                spot = (kind * 2 + tap) * chans
-                place = slice(spot, spot + chans)
-                weight_ref[place, :] = part if t == 0 else weight_ref[place, :] + part
+                add_weight(kind * 2 + tap, part, t == 0)
         into = nt(held_ref[...], taps_ref[...])
-        early = into[:, :chans]
+        before = into[:, :chans]
         if t > 0:
-            early = early + carried
-        grad_ref[:, at] = early.astype(BF16)
+            before = before + carried
+        grad_ref[:, at] = before.astype(BF16)
         carried = into[:, chans:] + cot.astype(F32)
     grad_ref[:, features:] = carried.astype(BF16)
+
+    for copy in early:
+        copy.wait_recv()
+    for t, at in enumerate(spans):
+        last_ref[...] = (hop_sum[:, at] + nn(far_ref[...], in_ref[:, at])).astype(BF16)
+        layer_ref[t] = (layer_sum[:, at] + nn(last_ref[...], mix_ref[2])).astype(BF16)
+        add_weight(6, tn(last_ref[...], cot_ref[t]), t == 0)
+    for copy in late + early:
+        copy.wait_send()
 
 
 def stages_of(axis_sizes):
@@ -423,7 +484,7 @@
     features = out_steps * chans
     n_dom, cap = send_rows.shape
     hub_per = hub_rows.shape[1]
-    width = cap + hub_per
+    width = -(-(cap + hub_per) // 16) * 16
     slots = n_dom * width
     block = tile_vals.shape[1]
     all_tiles = (nodes + n_dom * cap + hub_rows.size) // block
@@ -477,9 +538,11 @@
         halo,
     )
 
-    in_one = lax.all_to_all(out_one, "dom", split_axis=0, concat_axis=0, tiled=True)
+    sems = pltpu.SemaphoreType.DMA((2, n_dom - 1))
+    landing = pltpu.VMEM((slots, 2 * features), BF16)
+    partial = pltpu.VMEM((nodes, features), F32)
     hop_one, back_one, out_two = pl.pallas_call(
-        mid_kernel,
+        functools.partial(mid_kernel, n_dom),
         out_shape=(
             shape_of(nodes, features),
             shape_of(nodes, features),
@@ -487,11 +550,12 @@
         ),
         in_specs=[VMEM] * 8,
         out_specs=(VMEM,) * 3,
+        scratch_shapes=[landing, partial, partial, sems, sems],
+        compiler_params=pltpu.CompilerParams(collective_id=1, has_side_effects=True),
         name="mid",
-    )(own, far, send, hidden, back_two, cot, mix_weight, in_one)
-    in_two = lax.all_to_all(out_two, "dom", split_axis=0, concat_axis=0, tiled=True)
+    )(own, far, send, hidden, back_two, cot, mix_weight, out_one)
     layer_out, signal_grad, grads = pl.pallas_call(
-        post_kernel,
+        functools.partial(post_kernel, n_dom),
         out_shape=(
             shape_of(out_steps, nodes, chans),
             shape_of(nodes, steps * chans),
@@ -500,10 +564,17 @@
         in_specs=[VMEM] * 13,
         out_specs=(VMEM,) * 3,
         scratch_shapes=[
+            landing,
+            partial,
+            partial,
+            partial,
             pltpu.VMEM((2 * chans, 2 * chans), BF16),
             pltpu.VMEM((nodes, chans), BF16),
             pltpu.VMEM((nodes, 2 * chans), BF16),
+            sems,
+            sems,
         ],
+        compiler_params=pltpu.CompilerParams(collective_id=2, has_side_effects=True),
         name="post",
     )(
         own,
@@ -512,7 +583,7 @@
         hidden,
         hop_one,
         back_one,
-        in_two,
+        out_two,
         sig,
         cot,
         tanh_filt,

time: 119 us -> 109 us (0.916)
  blocking collectives: 51.1 us -> 0 us
  Pallas kernels: 59.8 us -> 100 us
    all_to_all x2 -> x0, blocking collectives: 51.1 us -> none  [the longest x1 27.6 us: body(): lax.all_to_all(out_one, 'dom', split_axis=0, concat_axis=0, tiled=True)]
    pallas_call x2, Pallas kernels: 15.5 us -> 53.9 us  [the longest x1 28.5 us: body(): pl.pallas_call(functools.partial(post_kernel, n_dom), out_shape=(shape_of...]
    pallas_call x1, Pallas kernels: 38 us -> 40.2 us  [reduce_weights(): pl.pallas_call(functools.partial(reduce_kernel, colours, factor), out_sha...]
    unnamed x3 -> x6, local copies, waits for them, and re-layouts: 2.43 us -> 3.31 us
where the time goes in v3:
time: 109 us
  Pallas kernels  100 us (92%)
  local copies, waits for them, and re-layouts  5.85 us (5%)
  other arithmetic  2 us (2%)
    pallas_call x1, Pallas kernels, reduce_weights(): pl.pallas_call(functools.partial(reduce_kernel, colours, factor), out_sha...  40.2 us
    pallas_call x1, Pallas kernels, body(): pl.pallas_call(functools.partial(post_kernel, n_dom), out_shape=(shape_of...  28.5 us
    pallas_call x1, Pallas kernels, body(): pl.pallas_call(functools.partial(mid_kernel, n_dom), out_shape=(shape_of(...  25.4 us
    pallas_call x1, Pallas kernels, body(): pl.pallas_call(pre_kernel, out_shape=(shape_of(nodes, nodes), shape_of(no...  6.32 us
    unnamed x6, local copies, waits for them, and re-layouts  3.31 us

profile of v3, /device:TPU:0, one launch (start us, length us, event | category | flops | bytes accessed | tf_op | source)
XLA Modules:
  0.0 108.9 jit_solution(16020776902030150691)
XLA Ops:
  0.6 2.4 %copy.20 = bf16[64,8,4,256]{3,1,2,0:T(8,128)(2,1)} copy(bf16[64,8,4,256]{3,2,1,0:T(4,128)(2,1)} %bitcast.21) | data formatting | bytes 2097152
  3.1 6.3 %pre.1 = (bf16[512,512]{1,0:T(8,128)(2,1)}, bf16[512,256]{1,0:T(8,128)(2,1)}, bf16[256,512]{1,0:T(8,128)(2,1)}, bf16[512,768]{1,0:T(8,128)(2,1)}, f32[512,768]{1...) custom-call(s32[16]{0:T(128)} %row_ref.1, s32[16]{0:T(128)} %col_ref.1, ...), custom_call_target="tpu_custom_call" | custom-call | tf_op jit(solution)/shard_map/pre/pallas_call | solution.py:503
  9.4 25.4 %mid.1 = (bf16[512,768]{1,0:T(8,128)(2,1)}, bf16[512,768]{1,0:T(8,128)(2,1)}, bf16[256,1536]{1,0:T(8,128)(2,1)}) custom-call(bf16[512,512]{1,0:T(8,128)(2,1)} %get-tuple-element.18.own_ref, bf16[512,256]{1,0:T(8,128)(2,1)} %get-tuple-element.19.far_ref, bf16[256,512]{1,0:T(8,128)(2,1)} %get-tuple-element.20.send_ref, ...), custom_call_target="tpu_custom_call" | custom-call | tf_op jit(solution)/shard_map/mid/pallas_call | solution.py:544
  34.8 28.5 %post.1 = (bf16[3,512,256]{2,1,0:T(8,128)(2,1)}, bf16[512,1024]{1,0:T(8,128)(2,1)}, f32[1792,256]{1,0:T(8,128)}) custom-call(bf16[512,512]{1,0:T(8,128)(2,1)} %get-tuple-element.18.own_ref, bf16[512,256]{1,0:T(8,128)(2,1)} %get-tuple-element.19.far_ref, bf16[256,512]{1,0:T(8,128)(2,1)} %get-tuple-element.20.send_ref, ...), custom_call_target="tpu_custom_call" | custom-call | tf_op jit(solution)/shard_map/post/pallas_call | solution.py:557
  63.3 40.2 %reduce_weights.1 = bf16[1792,256]{1,0:T(8,128)(2,1)} custom-call(f32[1792,256]{1,0:T(8,128)} %get-tuple-element.31.grads_ref), custom_call_target="tpu_custom_call" | custom-call | tf_op jit(solution)/shard_map/reduce_weights/pallas_call | solution.py:443
  103.4 0.0 slice-start
  103.5 0.0 slice-start.1
  103.5 0.0 copy-start
  103.5 1.0 slice-done
  104.4 0.9 convert.3
  105.4 0.0 slice-done.1
  105.4 0.0 copy-start.1
  105.4 1.1 convert.2
  106.5 0.0 copy-done
  106.5 1.6 %reshape.35 = bf16[512,1,4,256]{3,2,0,1:T(4,128)(2,1)} reshape(bf16[512,1024]{1,0:T(8,128)(2,1)S(1)} %copy-done) | data formatting | bytes 2097152 | tf_op jit(solution)/shard_map/reshape | solution.py:600
  108.0 0.0 copy-done.1
  108.0 0.9 copy.22
Async XLA Ops:
  103.4 1.0 slice-start
  103.5 1.9 %slice-start.1 = ((bf16[1792,256]{1,0:T(8,128)(2,1)}), bf16[1024,256]{1,0:T(8,128)(2,1)S(1)}, s32[]{:S(2)}) async-start(bf16[1792,256]{1,0:T(8,128)(2,1)} %reduce_weights.1), calls=%async_computation.1 | async-start | bytes 1048576 | tf_op jit(solution)/shard_map/slice | solution.py:601
  103.5 3.0 %copy-start = (bf16[512,1024]{1,0:T(8,128)(2,1)S(1)}, bf16[512,1024]{1,0:T(8,128)(2,1)}, u32[]{:S(2)}) copy-start(bf16[512,1024]{1,0:T(8,128)(2,1)} %get-tuple-element.30) | copy-start | bytes 3145732
  105.4 2.6 %copy-start.1 = (bf16[3,512,256]{2,1,0:T(8,128)(2,1)S(1)}, bf16[3,512,256]{2,1,0:T(8,128)(2,1)}, u32[]{:S(2)}) copy-start(bf16[3,512,256]{2,1,0:T(8,128)(2,1)} %get-tuple-element.29) | copy-start | bytes 2359300

commit v4 on v3

--- a/solution.py
+++ b/solution.py
@@ -298,57 +298,60 @@
         copy.wait_send()
 
 
-def stages_of(axis_sizes):
-    bits = {}
-    for axis, size in axis_sizes:
-        bit = 1
-        while bit < size:
-            bits.setdefault(axis, []).append((axis, bit))
-            bit *= 2
-    return bits
-
-
-def colours_of(bits, rows, chans):
-    dom, batch = bits["dom"], bits["batch"]
-    first, far = batch[:1], batch[1:]
-    near, high = dom[:1], dom[1:]
-    orders = (
-        first + far + near + high,
-        first + near + high + far,
-        first + high + far + near,
-    )
-    units = rows // chans
-    shares = [units - 2 * (units // 3), units // 3, units // 3]
-    colours, base = [], 0
-    for order, share in zip(orders, shares):
-        plan, count = [], share * chans
-        for axis, bit in order:
-            halve = (count // 2) % 16 == 0
-            plan.append((axis, bit, halve, count // 2 if halve else count))
-            if halve:
-                count //= 2
-        colours.append((base, share * chans, plan))
-        base += share * chans
+def pairs_of(axis, size):
+    stages, stride = [], 1
+    while stride < size:
+        stages.append((axis, stride, 2))
+        stride *= 2
+    return stages
+
+
+def plan_of(order, rows):
+    plan, count = [], rows
+    for axis, stride, size in order:
+        split = count % (size * 16) == 0
+        if split:
+            count //= size
+        plan.append((axis, stride, size, split, count))
+    return plan
+
+
+def colours_of(axis_sizes, rows, chans):
+    sizes = dict(axis_sizes)
+    batch = pairs_of("batch", sizes["batch"])
+    first, rest = batch[:1], batch[1:]
+    direct = [("dom", 1, sizes["dom"])]
+    pairs = pairs_of("dom", sizes["dom"])
+    share = (rows // chans + 1) // 2 * chans
+    for middle in (direct, pairs):
+        colours = [
+            (0, share, plan_of(first + rest + middle, share)),
+            (share, rows - share, plan_of(first + middle + rest, rows - share)),
+        ]
+        if all(split or size == 2 for _, _, plan in colours for _, _, size, split, _ in plan):
+            break
     return colours
 
 
-def partner_of(axis, bit):
-    index = lax.axis_index(axis)
-    mine = (index // bit) % 2
-    return mine, index + bit - 2 * bit * mine
-
-
-def narrow(stage):
-    return stage in (1, 2)
+def narrow(stage, split):
+    return split and stage in (1, 2)
 
 
 def landing_rows(colours, wanted):
     return sum(
-        count
+        count * (size - 1)
         for _, _, plan in colours
-        for stage, (_, _, _, count) in enumerate(plan)
-        if narrow(stage) == wanted
-    )
+        for stage, (_, _, size, split, count) in enumerate(plan)
+        if narrow(stage, split) == wanted
+    )
+
+
+def others_of(axis, stride, size):
+    index = lax.axis_index(axis)
+    place = lax.rem(lax.div(index, stride), size)
+    base = index - place * stride
+    seats = [lax.rem(place + d, size) for d in range(1, size)]
+    return place, [(seat, base + seat * stride) for seat in seats]
 
 
 def reduce_kernel(
@@ -366,13 +369,13 @@
     back_recv,
 ):
     barrier = pltpu.get_barrier_semaphore()
-    peers = sorted({(axis, bit) for axis, bit, _, _ in colours[0][2]})
-    for axis, bit in peers:
-        _, other = partner_of(axis, bit)
-        pl.semaphore_signal(
-            barrier, inc=1, device_id={axis: other}, device_id_type=pl.DeviceIdType.MESH
-        )
-    pl.semaphore_wait(barrier, len(peers))
+    peers = sorted({(axis, stride, size) for axis, stride, size, _, _ in colours[0][2]})
+    for axis, stride, size in peers:
+        for _, other in others_of(axis, stride, size)[1]:
+            pl.semaphore_signal(
+                barrier, inc=1, device_id={axis: other}, device_id_type=pl.DeviceIdType.MESH
+            )
+    pl.semaphore_wait(barrier, sum(size - 1 for _, _, size in peers))
 
     starts = [base for base, _, _ in colours]
     trail = [[] for _ in colours]
@@ -380,65 +383,73 @@
     depth = len(colours[0][2])
     for s in range(depth):
         moves = []
-        small = narrow(s)
-        landing = landed if small else wide
         for c, (_, _, plan) in enumerate(colours):
-            axis, bit, halve, count = plan[s]
-            mine, other = partner_of(axis, bit)
+            axis, stride, size, split, count = plan[s]
+            small = narrow(s, split)
+            landing = landed if small else wide
+            place, others = others_of(axis, stride, size)
             source = grads_ref if s == 0 else total
-            keep = starts[c] + mine * count if halve else starts[c]
-            give = starts[c] + (1 - mine) * count if halve else starts[c]
-            give_rows = pl.ds(pl.multiple_of(give, 16), count)
+            keep = starts[c] + place * count if split else starts[c]
             keep_rows = pl.ds(pl.multiple_of(keep, 16), count)
-            spot = pl.ds(used[small], count)
-            if small:
-                leaving[spot, :] = source[give_rows, :].astype(BF16)
-            copy = pltpu.make_async_remote_copy(
-                src_ref=leaving.at[spot] if small else source.at[give_rows],
-                dst_ref=landing.at[spot],
-                send_sem=send_sem.at[c, s],
-                recv_sem=recv_sem.at[c, s],
-                device_id={axis: other},
-                device_id_type=pl.DeviceIdType.MESH,
-            )
-            copy.start()
-            moves.append((copy, source, keep_rows, spot))
-            used[small] += count
+            arrivals = []
+            for d, (seat, other) in enumerate(others):
+                give = starts[c] + seat * count if split else starts[c]
+                give_rows = pl.ds(pl.multiple_of(give, 16), count)
+                spot = pl.ds(used[small], count)
+                if small:
+                    leaving[spot, :] = source[give_rows, :].astype(BF16)
+                copy = pltpu.make_async_remote_copy(
+                    src_ref=leaving.at[spot] if small else source.at[give_rows],
+                    dst_ref=landing.at[spot],
+                    send_sem=send_sem.at[c, s, d],
+                    recv_sem=recv_sem.at[c, s, d],
+                    device_id={axis: other},
+                    device_id_type=pl.DeviceIdType.MESH,
+                )
+                copy.start()
+                arrivals.append((copy, spot))
+                used[small] += count
+            moves.append((arrivals, landing, source, keep_rows))
             trail[c].append(keep)
             starts[c] = keep
-        for copy, source, keep_rows, spot in moves:
-            copy.wait()
-            total[keep_rows, :] = source[keep_rows, :] + landing[spot, :].astype(F32)
+        for arrivals, landing, source, keep_rows in moves:
+            for copy, _ in arrivals:
+                copy.wait()
+            value = source[keep_rows, :]
+            for _, spot in arrivals:
+                value = value + landing[spot, :].astype(F32)
+            total[keep_rows, :] = value
 
     for c, (_, _, plan) in enumerate(colours):
-        rows = pl.ds(pl.multiple_of(starts[c], 16), plan[-1][3])
+        rows = pl.ds(pl.multiple_of(starts[c], 16), plan[-1][4])
         out_ref[rows, :] = (total[rows, :] * factor).astype(BF16)
     for s in range(depth - 1, -1, -1):
         moves = []
         for c, (_, _, plan) in enumerate(colours):
-            axis, bit, halve, count = plan[s]
-            if not halve:
+            axis, stride, size, split, count = plan[s]
+            if not split:
                 continue
-            _, other = partner_of(axis, bit)
             rows = pl.ds(pl.multiple_of(trail[c][s], 16), count)
-            copy = pltpu.make_async_remote_copy(
-                src_ref=out_ref.at[rows],
-                dst_ref=out_ref.at[rows],
-                send_sem=back_send.at[c, s],
-                recv_sem=back_recv.at[c, s],
-                device_id={axis: other},
-                device_id_type=pl.DeviceIdType.MESH,
-            )
-            copy.start()
-            moves.append(copy)
+            for d, (_, other) in enumerate(others_of(axis, stride, size)[1]):
+                copy = pltpu.make_async_remote_copy(
+                    src_ref=out_ref.at[rows],
+                    dst_ref=out_ref.at[rows],
+                    send_sem=back_send.at[c, s, d],
+                    recv_sem=back_recv.at[c, s, d],
+                    device_id={axis: other},
+                    device_id_type=pl.DeviceIdType.MESH,
+                )
+                copy.start()
+                moves.append(copy)
         for copy in moves:
             copy.wait()
 
 
 def reduce_weights(grads, axis_sizes, factor, chans):
     rows, lanes = grads.shape
-    colours = colours_of(stages_of(axis_sizes), rows, chans)
-    sems = pltpu.SemaphoreType.DMA((len(colours), len(colours[0][2])))
+    colours = colours_of(axis_sizes, rows, chans)
+    most = max(size for _, _, size, _, _ in colours[0][2]) - 1
+    sems = pltpu.SemaphoreType.DMA((len(colours), len(colours[0][2]), most))
     slim = landing_rows(colours, True)
     return pl.pallas_call(
         functools.partial(reduce_kernel, colours, factor),

time: 109 us -> 103 us (0.945)
  Pallas kernels: 100 us -> 93.8 us
    pallas_call x1, Pallas kernels: 40.2 us -> 33.7 us  [reduce_weights(): pl.pallas_call(functools.partial(reduce_kernel, colours, factor), out_sha...]
where the time goes in v4:
time: 103 us; the launch traced here: 102 us
  Pallas kernels  93.8 us (91%)
  local copies, waits for them, and re-layouts  5.85 us (6%)
  other arithmetic  2 us (2%)
    pallas_call x1, Pallas kernels, reduce_weights(): pl.pallas_call(functools.partial(reduce_kernel, colours, factor), out_sha...  33.7 us
    pallas_call x1, Pallas kernels, body(): pl.pallas_call(functools.partial(post_kernel, n_dom), out_shape=(shape_of...  28.5 us
    pallas_call x1, Pallas kernels, body(): pl.pallas_call(functools.partial(mid_kernel, n_dom), out_shape=(shape_of(...  25.4 us
    pallas_call x1, Pallas kernels, body(): pl.pallas_call(pre_kernel, out_shape=(shape_of(nodes, nodes), shape_of(no...  6.33 us
    unnamed x6, local copies, waits for them, and re-layouts  3.31 us

profile of v4, /device:TPU:0, one launch (start us, length us, event | category | flops | bytes accessed | tf_op | source)
XLA Modules:
  0.0 102.4 jit_solution(17567077964086703652)
XLA Ops:
  0.6 2.4 %copy.20 = bf16[64,8,4,256]{3,1,2,0:T(8,128)(2,1)} copy(bf16[64,8,4,256]{3,2,1,0:T(4,128)(2,1)} %bitcast.21) | data formatting | bytes 2097152
  3.1 6.3 %pre.1 = (bf16[512,512]{1,0:T(8,128)(2,1)}, bf16[512,256]{1,0:T(8,128)(2,1)}, bf16[256,512]{1,0:T(8,128)(2,1)}, bf16[512,768]{1,0:T(8,128)(2,1)}, f32[512,768]{1...) custom-call(s32[16]{0:T(128)} %row_ref.1, s32[16]{0:T(128)} %col_ref.1, ...), custom_call_target="tpu_custom_call" | custom-call | tf_op jit(solution)/shard_map/pre/pallas_call | solution.py:514
  9.4 25.4 %mid.1 = (bf16[512,768]{1,0:T(8,128)(2,1)}, bf16[512,768]{1,0:T(8,128)(2,1)}, bf16[256,1536]{1,0:T(8,128)(2,1)}) custom-call(bf16[512,512]{1,0:T(8,128)(2,1)} %get-tuple-element.18.own_ref, bf16[512,256]{1,0:T(8,128)(2,1)} %get-tuple-element.19.far_ref, bf16[256,512]{1,0:T(8,128)(2,1)} %get-tuple-element.20.send_ref, ...), custom_call_target="tpu_custom_call" | custom-call | tf_op jit(solution)/shard_map/mid/pallas_call | solution.py:555
  34.8 28.5 %post.1 = (bf16[3,512,256]{2,1,0:T(8,128)(2,1)}, bf16[512,1024]{1,0:T(8,128)(2,1)}, f32[1792,256]{1,0:T(8,128)}) custom-call(bf16[512,512]{1,0:T(8,128)(2,1)} %get-tuple-element.18.own_ref, bf16[512,256]{1,0:T(8,128)(2,1)} %get-tuple-element.19.far_ref, bf16[256,512]{1,0:T(8,128)(2,1)} %get-tuple-element.20.send_ref, ...), custom_call_target="tpu_custom_call" | custom-call | tf_op jit(solution)/shard_map/post/pallas_call | solution.py:568
  63.3 33.7 %reduce_weights.1 = bf16[1792,256]{1,0:T(8,128)(2,1)} custom-call(f32[1792,256]{1,0:T(8,128)} %get-tuple-element.31.grads_ref), custom_call_target="tpu_custom_call" | custom-call | tf_op jit(solution)/shard_map/reduce_weights/pallas_call | solution.py:454
  96.9 0.0 slice-start
  96.9 0.0 slice-start.1
  96.9 0.0 copy-start
  97.0 1.0 slice-done
  97.9 0.9 convert.3
  98.9 0.0 slice-done.1
  98.9 0.0 copy-start.1
  98.9 1.1 %convert.2 = f32[2,2,256,256]{3,2,1,0:T(8,128)} convert(bf16[2,2,256,256]{3,2,1,0:T(8,128)(2,1)S(1)} %bitcast.20) | non-fusion elementwise | flops 262144 | bytes 1572864 | tf_op jit(solution)/shard_map/reshape | solution.py:612
  99.9 0.0 copy-done
  99.9 1.6 %reshape.35 = bf16[512,1,4,256]{3,2,0,1:T(4,128)(2,1)} reshape(bf16[512,1024]{1,0:T(8,128)(2,1)S(1)} %copy-done) | data formatting | bytes 2097152 | tf_op jit(solution)/shard_map/reshape | solution.py:611
  101.5 0.0 copy-done.1
  101.5 0.9 copy.22
Async XLA Ops:
  96.9 1.0 slice-start
  96.9 1.9 %slice-start.1 = ((bf16[1792,256]{1,0:T(8,128)(2,1)}), bf16[1024,256]{1,0:T(8,128)(2,1)S(1)}, s32[]{:S(2)}) async-start(bf16[1792,256]{1,0:T(8,128)(2,1)} %reduce_weights.1), calls=%async_computation.1 | async-start | bytes 1048576 | tf_op jit(solution)/shard_map/slice | solution.py:612
  96.9 3.0 %copy-start = (bf16[512,1024]{1,0:T(8,128)(2,1)S(1)}, bf16[512,1024]{1,0:T(8,128)(2,1)}, u32[]{:S(2)}) copy-start(bf16[512,1024]{1,0:T(8,128)(2,1)} %get-tuple-element.30) | copy-start | bytes 3145732
  98.9 2.6 %copy-start.1 = (bf16[3,512,256]{2,1,0:T(8,128)(2,1)S(1)}, bf16[3,512,256]{2,1,0:T(8,128)(2,1)}, u32[]{:S(2)}) copy-start(bf16[3,512,256]{2,1,0:T(8,128)(2,1)} %get-tuple-element.29) | copy-start | bytes 2359300
